TPU v7x, 32 devices: a whole 2x2x4 slice. The times are simulated.
32 devices in a mesh: atm: 8 (over z, y), ocn: 4 (over x, core).
Axes of the slice: x: 2, y: 2, z: 4, core: 2. Of those that a mesh axis runs over, the one named last changes fastest.
Arguments:
- atm_fields: bfloat16 [4096, 24, 128], P(('atm', 'ocn')), may hold values from -6 to 6
- fwd_blocks: bfloat16 [6144, 128, 128], P(('atm', 'ocn')), may hold values from -0.21875 to 0.21875
- fwd_src_tile: int32 [6144], P(('atm', 'ocn')), may hold values from 0 to 127
- fwd_dst_dev: int32 [6144, 1], P(('atm', 'ocn')), may hold values from 0 to 31, as said below
- fwd_dst_tile: int32 [6144], P(('atm', 'ocn')), may hold values from 0 to 7
- ocean_state: float32 [256, 24, 128], P(('atm', 'ocn')), may hold values from -6 to 6
- wet_mask: int32 [256, 128], P(('atm', 'ocn')), may hold values 0 or 1
- back_blocks: bfloat16 [6144, 128, 128], P(('atm', 'ocn')), may hold values from -0.3125 to 0.3125
- back_src_dev: int32 [6144, 1], P(('atm', 'ocn')), may hold values from 0 to 31, as said below
- back_src_tile: int32 [6144], P(('atm', 'ocn')), may hold values from 0 to 7
- back_dst_tile: int32 [6144], P(('atm', 'ocn')), may hold values from 0 to 127
Outputs:
- ocean_import: float32 [256, 24, 128], P(('atm', 'ocn'))
- atm_import: float32 [4096, 24, 128], P(('atm', 'ocn'))
Inputs may be any that keep to these rules, and one draw needn't show every extreme that they name: `fwd_dst_dev`: device d has atm index d // 4 and ocn index d % 4; the device named by a block of device b // 192 differs from it by at most one in each index, counted with wrap-around (nine neighbours, itself included). Among the 192 blocks of one device at most 48 name the same device, and on every device exactly one device is named 48 times. `back_src_dev`: device d has atm index d // 4 and ocn index d % 4; the device named by a block of device b // 192 differs from it by at most one in each index, counted with wrap-around (nine neighbours, itself included). Among the 192 blocks of one device at most 48 name the same device, and on every device exactly one device is named 48 times.
All inputs are finite; a program needn't handle non-finite values. No bound on the sum of `wet_mask` on one device may be relied on, other than what follows from the above.
Results may differ from a plain program's by a relative error of at most 0.0022.
Values may be sent and summed in bfloat16 or wider, within the bound.
No kernel may reach another device: no remote copies, remote signals or barrier semaphores. Data moves between devices by JAX's collectives and lax.ppermute only.
A program may use at most 128 MiB of HBM per device.

v0:
```python
import jax
import jax.numpy as jnp
from jax import lax
from jax.sharding import PartitionSpec as P


def extended(block, sides, width):
    for axis, dim in sides:
        count = lax.axis_size(axis)
        forward = [(i, i + 1) for i in range(count - 1)]
        forward.append((count - 1, 0))
        backward = [(target, source) for source, target in forward]
        low = lax.ppermute(
            lax.slice_in_dim(block, block.shape[dim] - width, None, axis=dim), axis, forward
        )
        high = lax.ppermute(lax.slice_in_dim(block, 0, width, axis=dim), axis, backward)
        block = jnp.concatenate([low, block, high], axis=dim)
    return block


def tile_sums(labels, values, tiles):
    select = (labels[None, :] == jnp.arange(tiles, dtype=jnp.int32)[:, None]).astype(jnp.float32)
    flat = values.reshape(values.shape[0], -1)
    return jnp.dot(
        select, flat, precision=lax.Precision.HIGHEST, preferred_element_type=jnp.float32
    )


def neighbour_steps(owner, n_atmos, n_ocean):
    here_row = lax.axis_index("atm")
    here_col = lax.axis_index("ocn")
    rel_row = (owner // n_ocean - here_row) % n_atmos
    rel_col = (owner % n_ocean - here_col) % n_ocean
    row_step = jnp.where(rel_row == n_atmos - 1, 0, jnp.where(rel_row == 0, 1, 2)).astype(jnp.int32)
    col_step = jnp.where(rel_col == n_ocean - 1, 0, jnp.where(rel_col == 0, 1, 2)).astype(jnp.int32)
    return (row_step, col_step)


def shards(
    atm_fields,
    fwd_blocks,
    fwd_src_tile,
    fwd_dst_dev,
    fwd_dst_tile,
    ocean_state,
    wet_mask,
    back_blocks,
    back_src_dev,
    back_src_tile,
    back_dst_tile,
):
    n_atmos = lax.axis_size("atm")
    n_ocean = lax.axis_size("ocn")
    fields = atm_fields.shape[1]
    cells = atm_fields.shape[2]
    ocean_count = ocean_state.shape[0]
    atmos_count = atm_fields.shape[0]
    row_step, col_step = neighbour_steps(fwd_dst_dev[:, 0], n_atmos, n_ocean)
    neighbour = row_step * 3 + col_step
    sources = atm_fields[fwd_src_tile]
    fwd_part = jnp.einsum("bfi,bij->bfj", sources, fwd_blocks, preferred_element_type=jnp.float32)
    keyed = neighbour * ocean_count + fwd_dst_tile
    totals = tile_sums(keyed, fwd_part, 9 * ocean_count).reshape(3, 3, ocean_count, fields, cells)
    padded = extended(totals, (("atm", 0), ("ocn", 1)), 1)
    ocean_import = jnp.sum(padded[::2, ::2], axis=(0, 1))
    wet = wet_mask.astype(jnp.float32)[:, None, :]
    response = (wet * jnp.tanh(ocean_state + ocean_import)).astype(jnp.bfloat16)
    source_owner = back_src_dev[:, 0]
    back_row, back_col = neighbour_steps(source_owner, n_atmos, n_ocean)
    nearby = extended(response[None, None], (("atm", 0), ("ocn", 1)), 1)
    fetched = nearby.reshape(9 * ocean_count, fields, cells)[
        (back_row * 3 + back_col) * ocean_count + back_src_tile
    ]
    back_part = jnp.einsum("bfi,bij->bfj", fetched, back_blocks, preferred_element_type=jnp.float32)
    atm_import = tile_sums(back_dst_tile, back_part, atmos_count).reshape(
        atmos_count, fields, cells
    )
    return (ocean_import, atm_import)


def solution(mesh):
    in_specs = (
        P(("atm", "ocn"), None, None),
        P(("atm", "ocn"), None, None),
        P(("atm", "ocn")),
        P(("atm", "ocn"), None),
        P(("atm", "ocn")),
        P(("atm", "ocn"), None, None),
        P(("atm", "ocn"), None),
        P(("atm", "ocn"), None, None),
        P(("atm", "ocn"), None),
        P(("atm", "ocn")),
        P(("atm", "ocn")),
    )
    out_specs = (P(("atm", "ocn"), None, None), P(("atm", "ocn"), None, None))
    return jax.shard_map(shards, mesh=mesh, in_specs=in_specs, out_specs=out_specs, check_vma=False)
```

profile of v0, /device:TPU:1, one launch (start us, length us, event | category | flops | bytes accessed | tf_op | source)
XLA Modules:
  0.0 59.9 jit_solution(9159723258944549959)
XLA Ops:
  0.6 0.8 %compare_select_fusion.1 = s32[192]{0:T(256)S(1)} fusion(s32[192]{0:T(256)} %param.13), kind=kLoop, calls=%fused_computation.31 | loop fusion | flops 576 | bytes 1536 | tf_op jit(solution)/shard_map/select_n | solution.py:60
  1.4 0.4 copy-done
  1.8 0.9 %gather_fusion = bf16[192,24,128]{2,1,0:T(8,128)(2,1)S(1)} fusion(bf16[128,24,128]{2,1,0:T(8,128)(2,1)S(1)} %copy-done, s32[1024]{0:T(1024)S(1)} %pad_clamp_fusion.1), kind=kCustom, calls=%fused_computation | custom fusion | bytes 2360064 | tf_op jit(solution)/shard_map/gather | solution.py:60
  2.7 3.8 %fusion.28 = f32[192,24,128]{2,1,0:T(8,128)S(1)} fusion(bf16[192,24,128]{2,1,0:T(8,128)(2,1)S(1)} %gather_fusion, bf16[192,128,128]{2,1,0:T(8,128)(2,1)} %param.12), kind=kOutput, calls=%fused_computation.76 | convolution fusion | flops 150994944 | bytes 9830400 | tf_op jit(solution)/shard_map/bfi,bij->bfj/dot_general | solution.py:61
  6.6 1.2 %fusion = f32[72,3072]{1,0:T(8,128)S(1)} fusion(f32[24,8,24,128]{3,2,1,0:T(8,128)S(1)} %bitcast.36, s32[192]{0:T(256)S(1)} %fusion.17), kind=kOutput, calls=%fused_computation.4 | convolution fusion | flops 509621760 | bytes 3244800 | tf_op jit(solution)/shard_map/dot_general | solution.py:24
  7.9 2.1 %collective-permute-start = (f32[1,3,8,24,128]{4,2,3,1,0:T(8,128)S(1)}, f32[1,3,8,24,128]{4,2,3,1,0:T(8,128)S(1)}, u32[]{:S(2)}, u32[]{:S(2)}) collective-permute-start(f32[1,3,8,24,128]{4,2,3,1,0:T(8,128)S(1)} %get-tuple-element.12), channel_id=1, source_target_pairs={{0,4},{4,8},{8,12},{12,16},{16,20},{20,24},{24,28},{28,0},{1,5},{5... | collective-permute-start | bytes 884744 | tf_op jit(solution)/shard_map/ppermute | solution.py:13
  10.0 3.1 %collective-permute-start.1 = (f32[1,3,8,24,128]{4,2,3,1,0:T(8,128)S(1)}, f32[1,3,8,24,128]{4,2,3,1,0:T(8,128)S(1)}, u32[]{:S(2)}, u32[]{:S(2)}) collective-permute-start(f32[1,3,8,24,128]{4,2,3,1,0:T(8,128)S(1)} %get-tuple-element.13), channel_id=1, source_target_pairs={{4,0},{8,4},{12,8},{16,12},{20,16},{24,20},{28,24},{0,28},{5,1},{9... | collective-permute-start | bytes 884744 | tf_op jit(solution)/shard_map/ppermute | solution.py:16
  13.1 8.9 %collective-permute-done = f32[1,3,8,24,128]{4,2,3,1,0:T(8,128)S(1)} collective-permute-done((f32[1,3,8,24,128]{4,2,3,1,0:T(8,128)S(1)}, f32[1,3,8,24,128]{4,2,3,1,0:T(8,128)S(1)}, u32[]{:S(2)}, u32[]{:S(2)}) %collective-permute-start) | collective-permute-done | bytes 294944 | tf_op jit(solution)/shard_map/ppermute | solution.py:13
  22.0 1.9 %collective-permute-done.1 = f32[1,3,8,24,128]{4,2,3,1,0:T(8,128)S(1)} collective-permute-done((f32[1,3,8,24,128]{4,2,3,1,0:T(8,128)S(1)}, f32[1,3,8,24,128]{4,2,3,1,0:T(8,128)S(1)}, u32[]{:S(2)}, u32[]{:S(2)}) %collective-permute-start.1) | collective-permute-done | bytes 294944 | tf_op jit(solution)/shard_map/ppermute | solution.py:16
  23.9 0.1 pad_maximum_fusion.3
  24.0 3.0 %collective-permute-start.2 = (f32[5,1,8,24,128]{4,2,3,1,0:T(8,128)S(1)}, f32[5,1,8,24,128]{4,2,3,1,0:T(8,128)S(1)}, u32[]{:S(2)}, u32[]{:S(2)}) collective-permute-start(f32[5,1,8,24,128]{4,2,3,1,0:T(8,128)S(1)} %get-tuple-element.10), channel_id=1, source_target_pairs={{0,1},{1,2},{2,3},{3,0},{4,5},{5,6},{6,7},{7,4},{8,9},{9,10},{10,1... | collective-permute-start | bytes 1474568 | tf_op jit(solution)/shard_map/ppermute | solution.py:13
  27.0 10.2 %collective-permute-done.2 = f32[5,1,8,24,128]{4,2,3,1,0:T(8,128)S(1)} collective-permute-done((f32[5,1,8,24,128]{4,2,3,1,0:T(8,128)S(1)}, f32[5,1,8,24,128]{4,2,3,1,0:T(8,128)S(1)}, u32[]{:S(2)}, u32[]{:S(2)}) %collective-permute-start.2) | collective-permute-done | bytes 491552 | tf_op jit(solution)/shard_map/ppermute | solution.py:13
  37.1 1.5 %collective-permute-done.3 = f32[5,1,8,24,128]{4,2,3,1,0:T(8,128)S(1)} collective-permute-done((f32[5,1,8,24,128]{4,2,3,1,0:T(8,128)S(1)}, f32[5,1,8,24,128]{4,2,3,1,0:T(8,128)S(1)}, u32[]{:S(2)}, u32[]{:S(2)}) %collective-permute-start.3) | collective-permute-done | bytes 491552 | tf_op jit(solution)/shard_map/ppermute | solution.py:16
  38.7 0.2 pad_maximum_fusion
  39.1 4.1 %collective-permute-start.5 = (bf16[1,1,8,24,128]{4,2,3,1,0:T(8,128)(2,1)S(1)}, bf16[1,1,8,24,128]{4,2,3,1,0:T(8,128)(2,1)S(1)}, u32[]{:S(2)}, u32[]{:S(2)}) collective-permute-start(bf16[1,1,8,24,128]{4,2,3,1,0:T(8,128)(2,1)S(1)} %fusion.11), channel_id=1, source_target_pairs={{4,0},{8,4},{12,8},{16,12},{20,16},{24,20},{28,24},{0,28},{5,1},{9... | collective-permute-start | bytes 147464 | tf_op jit(solution)/shard_map/ppermute | solution.py:16
  43.2 2.1 %collective-permute-done.4 = bf16[1,1,8,24,128]{4,2,3,1,0:T(8,128)(2,1)S(1)} collective-permute-done((bf16[1,1,8,24,128]{4,2,3,1,0:T(8,128)(2,1)S(1)}, bf16[1,1,8,24,128]{4,2,3,1,0:T(8,128)(2,1)S(1)}, u32[]{:S(2)}, u32[]{:S(2)}) %collective-permute-start.4) | collective-permute-done | bytes 49184 | tf_op jit(solution)/shard_map/ppermute | solution.py:13
  45.4 1.7 %collective-permute-start.6 = (bf16[3,1,8,24,128]{4,2,3,1,0:T(8,128)(2,1)S(1)}, bf16[3,1,8,24,128]{4,2,3,1,0:T(8,128)(2,1)S(1)}, u32[]{:S(2)}, u32[]{:S(2)}) collective-permute-start(bf16[3,1,8,24,128]{4,2,3,1,0:T(8,128)(2,1)S(1)} %pad_maximum_fusion.5), channel_id=1, source_target_pairs={{0,1},{1,2},{2,3},{3,0},{4,5},{5,6},{6,7},{7,4},{8,9},{9,10},{10,1... | collective-permute-start | bytes 442376 | tf_op jit(solution)/shard_map/ppermute | solution.py:13
  47.1 0.7 %copy.23 = f32[8,24,128]{2,1,0:T(8,128)} copy(f32[8,24,128]{2,0,1:T(8,128)S(1)} %slice_reduce_fusion) | data formatting | bytes 196608
  47.8 2.1 %collective-permute-done.6 = bf16[3,1,8,24,128]{4,2,3,1,0:T(8,128)(2,1)S(1)} collective-permute-done((bf16[3,1,8,24,128]{4,2,3,1,0:T(8,128)(2,1)S(1)}, bf16[3,1,8,24,128]{4,2,3,1,0:T(8,128)(2,1)S(1)}, u32[]{:S(2)}, u32[]{:S(2)}) %collective-permute-start.6) | collective-permute-done | bytes 147488 | tf_op jit(solution)/shard_map/ppermute | solution.py:13
  49.9 1.7 %collective-permute-done.7 = bf16[3,1,8,24,128]{4,2,3,1,0:T(8,128)(2,1)S(1)} collective-permute-done((bf16[3,1,8,24,128]{4,2,3,1,0:T(8,128)(2,1)S(1)}, bf16[3,1,8,24,128]{4,2,3,1,0:T(8,128)(2,1)S(1)}, u32[]{:S(2)}, u32[]{:S(2)}) %collective-permute-start.7) | collective-permute-done | bytes 147488 | tf_op jit(solution)/shard_map/ppermute | solution.py:16
  51.8 0.9 %gather_fusion.1 = bf16[192,24,128]{2,1,0:T(8,128)(2,1)S(1)} fusion(bf16[72,24,128]{2,1,0:T(8,128)(2,1)S(1)} %bitcast.38, s32[1024]{0:T(1024)S(1)} %pad_clamp_fusion), kind=kCustom, calls=%fused_computation.1 | custom fusion | bytes 2360064 | tf_op jit(solution)/shard_map/gather | solution.py:71
  52.7 3.8 %fusion.29 = f32[192,24,128]{2,1,0:T(8,128)S(1)} fusion(bf16[192,24,128]{2,1,0:T(8,128)(2,1)S(1)} %gather_fusion.1, bf16[192,128,128]{2,1,0:T(8,128)(2,1)} %param.18), kind=kOutput, calls=%fused_computation.77 | convolution fusion | flops 150994944 | bytes 9830400 | tf_op jit(solution)/shard_map/bfi,bij->bfj/dot_general | solution.py:74
  56.5 1.4 %fusion.3 = f32[128,24,128]{2,0,1:T(8,128)S(1)} fusion(s32[192]{0:T(256)S(1)} %copy-done.3, f32[24,8,24,128]{3,2,1,0:T(8,128)S(1)} %bitcast.37), kind=kOutput, calls=%fused_computation.7 | convolution fusion | flops 905994240 | bytes 3932928 | tf_op jit(solution)/shard_map/dot_general | solution.py:24
  57.9 2.1 %copy.24 = f32[128,24,128]{2,1,0:T(8,128)} copy(f32[128,24,128]{2,0,1:T(8,128)S(1)} %fusion.3) | data formatting | bytes 3145728
  (30 shorter events, 0.4 us)
Async XLA Ops:
  0.6 1.2 %copy-start = (bf16[128,24,128]{2,1,0:T(8,128)(2,1)S(1)}, bf16[128,24,128]{2,1,0:T(8,128)(2,1)}, u32[]{:S(2)}) copy-start(bf16[128,24,128]{2,1,0:T(8,128)(2,1)} %param.11) | copy-start | bytes 2359300
  2.7 3.8 %copy-start.4 = (s32[192]{0:T(256)S(1)}, s32[192]{0:T(256)}, u32[]{:S(2)}) copy-start(s32[192]{0:T(256)} %param.15) | copy-start | bytes 2308
  2.7 3.8 %copy-start.5 = (s32[192,1]{0,1:T(1,128)S(1)}, s32[192,1]{0,1:T(1,128)}, u32[]{:S(2)}) copy-start(s32[192,1]{0,1:T(1,128)} %param.14) | copy-start | bytes 2308
  7.8 19.1 %copy-start.2 = (s32[8,128]{1,0:T(8,128)S(1)}, s32[8,128]{1,0:T(8,128)}, u32[]{:S(2)}) copy-start(s32[8,128]{1,0:T(8,128)} %param.17) | copy-start | bytes 12292
  7.9 14.1 %collective-permute-start = (f32[1,3,8,24,128]{4,2,3,1,0:T(8,128)S(1)}, f32[1,3,8,24,128]{4,2,3,1,0:T(8,128)S(1)}, u32[]{:S(2)}, u32[]{:S(2)}) collective-permute-start(f32[1,3,8,24,128]{4,2,3,1,0:T(8,128)S(1)} %get-tuple-element.12), channel_id=1, source_target_pairs={{0,4},{4,8},{8,12},{12,16},{16,20},{20,24},{24,28},{28,0},{1,5},{5... | collective-permute-start | bytes 884744 | tf_op jit(solution)/shard_map/ppermute | solution.py:13
  10.0 13.9 %collective-permute-start.1 = (f32[1,3,8,24,128]{4,2,3,1,0:T(8,128)S(1)}, f32[1,3,8,24,128]{4,2,3,1,0:T(8,128)S(1)}, u32[]{:S(2)}, u32[]{:S(2)}) collective-permute-start(f32[1,3,8,24,128]{4,2,3,1,0:T(8,128)S(1)} %get-tuple-element.13), channel_id=1, source_target_pairs={{4,0},{8,4},{12,8},{16,12},{20,16},{24,20},{28,24},{0,28},{5,1},{9... | collective-permute-start | bytes 884744 | tf_op jit(solution)/shard_map/ppermute | solution.py:16
  24.0 13.2 %collective-permute-start.2 = (f32[5,1,8,24,128]{4,2,3,1,0:T(8,128)S(1)}, f32[5,1,8,24,128]{4,2,3,1,0:T(8,128)S(1)}, u32[]{:S(2)}, u32[]{:S(2)}) collective-permute-start(f32[5,1,8,24,128]{4,2,3,1,0:T(8,128)S(1)} %get-tuple-element.10), channel_id=1, source_target_pairs={{0,1},{1,2},{2,3},{3,0},{4,5},{5,6},{6,7},{7,4},{8,9},{9,10},{10,1... | collective-permute-start | bytes 1474568 | tf_op jit(solution)/shard_map/ppermute | solution.py:13
  26.9 11.7 %collective-permute-start.3 = (f32[5,1,8,24,128]{4,2,3,1,0:T(8,128)S(1)}, f32[5,1,8,24,128]{4,2,3,1,0:T(8,128)S(1)}, u32[]{:S(2)}, u32[]{:S(2)}) collective-permute-start(f32[5,1,8,24,128]{4,2,3,1,0:T(8,128)S(1)} %get-tuple-element.11), channel_id=1, source_target_pairs={{1,0},{2,1},{3,2},{0,3},{5,4},{6,5},{7,6},{4,7},{9,8},{10,9},{11,1... | collective-permute-start | bytes 1474568 | tf_op jit(solution)/shard_map/ppermute | solution.py:16
  26.9 12.0 %copy-start.1 = (f32[8,24,128]{2,1,0:T(8,128)S(1)}, f32[8,24,128]{2,1,0:T(8,128)}, u32[]{:S(2)}) copy-start(f32[8,24,128]{2,1,0:T(8,128)} %param.16) | copy-start | bytes 294916
  27.0 20.1 %copy-start.6 = (s32[192]{0:T(256)S(1)}, s32[192]{0:T(256)}, u32[]{:S(2)}) copy-start(s32[192]{0:T(256)} %param.20) | copy-start | bytes 2308
  27.0 20.1 %copy-start.7 = (s32[192,1]{0,1:T(1,128)S(1)}, s32[192,1]{0,1:T(1,128)}, u32[]{:S(2)}) copy-start(s32[192,1]{0,1:T(1,128)} %param.19) | copy-start | bytes 2308
  39.0 6.3 %collective-permute-start.4 = (bf16[1,1,8,24,128]{4,2,3,1,0:T(8,128)(2,1)S(1)}, bf16[1,1,8,24,128]{4,2,3,1,0:T(8,128)(2,1)S(1)}, u32[]{:S(2)}, u32[]{:S(2)}) collective-permute-start(bf16[1,1,8,24,128]{4,2,3,1,0:T(8,128)(2,1)S(1)} %fusion.11), channel_id=1, source_target_pairs={{0,4},{4,8},{8,12},{12,16},{16,20},{20,24},{24,28},{28,0},{1,5},{5... | collective-permute-start | bytes 147464 | tf_op jit(solution)/shard_map/ppermute | solution.py:13
  39.1 6.3 %collective-permute-start.5 = (bf16[1,1,8,24,128]{4,2,3,1,0:T(8,128)(2,1)S(1)}, bf16[1,1,8,24,128]{4,2,3,1,0:T(8,128)(2,1)S(1)}, u32[]{:S(2)}, u32[]{:S(2)}) collective-permute-start(bf16[1,1,8,24,128]{4,2,3,1,0:T(8,128)(2,1)S(1)} %fusion.11), channel_id=1, source_target_pairs={{4,0},{8,4},{12,8},{16,12},{20,16},{24,20},{28,24},{0,28},{5,1},{9... | collective-permute-start | bytes 147464 | tf_op jit(solution)/shard_map/ppermute | solution.py:16
  45.4 4.5 %collective-permute-start.6 = (bf16[3,1,8,24,128]{4,2,3,1,0:T(8,128)(2,1)S(1)}, bf16[3,1,8,24,128]{4,2,3,1,0:T(8,128)(2,1)S(1)}, u32[]{:S(2)}, u32[]{:S(2)}) collective-permute-start(bf16[3,1,8,24,128]{4,2,3,1,0:T(8,128)(2,1)S(1)} %pad_maximum_fusion.5), channel_id=1, source_target_pairs={{0,1},{1,2},{2,3},{3,0},{4,5},{5,6},{6,7},{7,4},{8,9},{9,10},{10,1... | collective-permute-start | bytes 442376 | tf_op jit(solution)/shard_map/ppermute | solution.py:13
  47.1 4.6 %collective-permute-start.7 = (bf16[3,1,8,24,128]{4,2,3,1,0:T(8,128)(2,1)S(1)}, bf16[3,1,8,24,128]{4,2,3,1,0:T(8,128)(2,1)S(1)}, u32[]{:S(2)}, u32[]{:S(2)}) collective-permute-start(bf16[3,1,8,24,128]{4,2,3,1,0:T(8,128)(2,1)S(1)} %pad_maximum_fusion.5), channel_id=1, source_target_pairs={{1,0},{2,1},{3,2},{0,3},{5,4},{6,5},{7,6},{4,7},{9,8},{10,9},{11,1... | collective-permute-start | bytes 442376 | tf_op jit(solution)/shard_map/ppermute | solution.py:16
  52.7 3.8 %copy-start.3 = (s32[192]{0:T(256)S(1)}, s32[192]{0:T(256)}, u32[]{:S(2)}) copy-start(s32[192]{0:T(256)} %param.21) | copy-start | bytes 2308
where the time goes:
time: 60.1 us; the launch traced here: 59.9 us
  waiting for transfers between devices  28.5 us (47%)
  starting transfers between devices  14.1 us (23%)
  matrix products  10.2 us (17%)
  local copies, waits for them, and re-layouts  5.05 us (8%)
  other arithmetic  1.27 us (2%)
  between operations  0.86 us (1%)
    ppermute x4, waiting for transfers between devices, extended(): lax.ppermute(lax.slice_in_dim(block, block.shape[dim] - width, None, axis...  23.3 us
    ppermute x4, starting transfers between devices, extended(): lax.ppermute(lax.slice_in_dim(block, 0, width, axis=dim), axis, backward)  7.26 us
    ppermute x4, starting transfers between devices, extended(): lax.ppermute(lax.slice_in_dim(block, block.shape[dim] - width, None, axis...  6.84 us
    ppermute x4, waiting for transfers between devices, extended(): lax.ppermute(lax.slice_in_dim(block, 0, width, axis=dim), axis, backward)  5.17 us
    dot_general x1, matrix products, shards(): jnp.einsum('bfi,bij->bfj', sources, fwd_blocks, preferred_element_type=jn...  3.78 us
    dot_general x1, matrix products, shards(): jnp.einsum('bfi,bij->bfj', fetched, back_blocks, preferred_element_type=j...  3.78 us
    unnamed x18, local copies, waits for them, and re-layouts  3.14 us
    dot_general x2, matrix products, tile_sums(): jnp.dot(select, flat, precision=lax.Precision.HIGHEST, preferred_element_...  2.59 us
  transfers between devices with their start and end apart: 8, of which 7 were waited for; matrix products, arithmetic and copies ran while one was open for 1% of the time, Pallas kernels for 0%

commit v1 on v0

v1 whole, which is shorter than its diff:
```python
import functools

import jax
import jax.numpy as jnp
from jax import lax
from jax.experimental import pallas as pl
from jax.experimental.pallas import tpu as pltpu
from jax.sharding import PartitionSpec as P

CHUNKS = 8
UNROLL = 8


def neighbour_ids(n_atmos, n_ocean):
    row, col = lax.axis_index("atm"), lax.axis_index("ocn")
    rows = [lax.rem(row + step + n_atmos, n_atmos) for step in (-1, 0, 1)]
    cols = [lax.rem(col + step + n_ocean, n_ocean) for step in (-1, 0, 1)]
    return [r * n_ocean + c for r in rows for c in cols]


def fill_table(table, n_atmos, n_ocean):
    for place, device in enumerate(neighbour_ids(n_atmos, n_ocean)):
        table[device] = place


def block_sums(blocks, source_of, target_of, load, total, chunk):
    def group(first, carry):
        at = first * UNROLL
        products = []
        for step in range(UNROLL):
            products.append(
                jnp.dot(load(source_of(at + step)), blocks[at + step], preferred_element_type=jnp.float32)
            )
        for step in range(UNROLL):
            target = target_of(at + step)
            total[target] = total[target] + products[step]
        return carry

    lax.fori_loop(chunk[0] // UNROLL, chunk[1] // UNROLL, group, 0)


def start_all(copies):
    for copy in copies:
        copy.start()
    return copies


def weight_copies(hbm, vmem, sems):
    count = hbm.shape[0] // CHUNKS
    return [
        pltpu.make_async_copy(
            hbm.at[pl.ds(c * count, count)], vmem.at[pl.ds(c * count, count)], sems.at[c]
        )
        for c in range(CHUNKS)
    ]


def fwd_kernel(
    n_atmos, n_ocean, fields_hbm, blocks_hbm, src_hbm, dev_hbm, tile_hbm, total,
    blocks, fields, src, dev, tile, table, sems, index_sems,
):
    tiles = total.shape[0] // 9
    small = start_all([
        pltpu.make_async_copy(src_hbm, src, index_sems.at[0]),
        pltpu.make_async_copy(dev_hbm, dev, index_sems.at[1]),
        pltpu.make_async_copy(tile_hbm, tile, index_sems.at[2]),
        pltpu.make_async_copy(fields_hbm, fields, index_sems.at[3]),
    ])
    weights = start_all(weight_copies(blocks_hbm, blocks, sems))
    fill_table(table, n_atmos, n_ocean)
    total[...] = jnp.zeros_like(total)
    for copy in small:
        copy.wait()
    count = blocks.shape[0] // CHUNKS
    for c in range(CHUNKS):
        weights[c].wait()
        block_sums(
            blocks, lambda b: src[b], lambda b: table[dev[b]] * tiles + tile[b],
            lambda s: fields[s], total, (c * count, (c + 1) * count),
        )


def bwd_kernel(
    n_atmos, n_ocean, near_ref, blocks, dev_hbm, src_hbm, dst_hbm, total,
    dev, src, dst, table, index_sems,
):
    tiles = near_ref.shape[0] // 9
    small = start_all([
        pltpu.make_async_copy(src_hbm, src, index_sems.at[0]),
        pltpu.make_async_copy(dev_hbm, dev, index_sems.at[1]),
        pltpu.make_async_copy(dst_hbm, dst, index_sems.at[2]),
    ])
    fill_table(table, n_atmos, n_ocean)
    total[...] = jnp.zeros_like(total)
    for copy in small:
        copy.wait()
    block_sums(
        blocks, lambda b: table[dev[b]] * tiles + src[b], lambda b: dst[b],
        lambda s: near_ref[s], total, (0, blocks.shape[0]),
    )


def in_hbm(*arrays):
    return [pltpu.with_memory_space_constraint(a, pltpu.HBM) for a in arrays]


def hbm():
    return pl.BlockSpec(memory_space=pl.ANY)


def vmem():
    return pl.BlockSpec(memory_space=pltpu.VMEM)


def forward(n_atmos, n_ocean, atm_fields, fwd_blocks, src, dev, tile, ocean_count):
    fields, cells = atm_fields.shape[1:]
    count = fwd_blocks.shape[0]
    return pl.pallas_call(
        functools.partial(fwd_kernel, n_atmos, n_ocean),
        out_shape=jax.ShapeDtypeStruct((9 * ocean_count, fields, cells), jnp.float32),
        in_specs=[hbm()] * 5,
        out_specs=vmem(),
        scratch_shapes=[
            pltpu.VMEM(fwd_blocks.shape, fwd_blocks.dtype),
            pltpu.VMEM(atm_fields.shape, atm_fields.dtype),
            pltpu.SMEM((count,), jnp.int32),
            pltpu.SMEM((count,), jnp.int32),
            pltpu.SMEM((count,), jnp.int32),
            pltpu.SMEM((n_atmos * n_ocean,), jnp.int32),
            pltpu.SemaphoreType.DMA((CHUNKS,)),
            pltpu.SemaphoreType.DMA((4,)),
        ],
        compiler_params=pltpu.CompilerParams(vmem_limit_bytes=16 * 2**20),
        name="forward_blocks",
    )(*in_hbm(atm_fields, fwd_blocks, src, dev, tile))


def backward(n_atmos, n_ocean, near, back_blocks, dev, src, dst, atmos_count):
    fields, cells = near.shape[1:]
    count = back_blocks.shape[0]
    return pl.pallas_call(
        functools.partial(bwd_kernel, n_atmos, n_ocean),
        out_shape=jax.ShapeDtypeStruct((atmos_count, fields, cells), jnp.float32),
        in_specs=[vmem()] * 2 + [hbm()] * 3,
        out_specs=vmem(),
        scratch_shapes=[
            pltpu.SMEM((count,), jnp.int32),
            pltpu.SMEM((count,), jnp.int32),
            pltpu.SMEM((count,), jnp.int32),
            pltpu.SMEM((n_atmos * n_ocean,), jnp.int32),
            pltpu.SemaphoreType.DMA((3,)),
        ],
        compiler_params=pltpu.CompilerParams(vmem_limit_bytes=16 * 2**20),
        name="backward_blocks",
    )(near, back_blocks, dev, src, dst)


def shift(block, axis, step):
    count = lax.axis_size(axis)
    return lax.ppermute(block, axis, [(i, (i + step) % count) for i in range(count)])


def gathered_sums(totals):
    for axis in ("ocn", "atm"):
        dim = totals.ndim - 4
        low, own, high = (lax.index_in_dim(totals, i, dim, keepdims=False) for i in range(3))
        from_high = shift(low.astype(jnp.float16), axis, -1)
        from_low = shift(high.astype(jnp.float16), axis, 1)
        totals = own + from_high.astype(jnp.float32) + from_low.astype(jnp.float32)
    return totals


def shards(
    atm_fields, fwd_blocks, fwd_src_tile, fwd_dst_dev, fwd_dst_tile, ocean_state, wet_mask,
    back_blocks, back_src_dev, back_src_tile, back_dst_tile,
):
    n_atmos = lax.axis_size("atm")
    n_ocean = lax.axis_size("ocn")
    fields, cells = atm_fields.shape[1:]
    ocean_count = ocean_state.shape[0]
    atmos_count = atm_fields.shape[0]
    totals = forward(
        n_atmos, n_ocean, atm_fields, fwd_blocks, fwd_src_tile, fwd_dst_dev[:, 0], fwd_dst_tile, ocean_count
    ).reshape(3, 3, ocean_count, fields, cells)
    ocean_import = gathered_sums(totals)
    wet = wet_mask.astype(jnp.float32)[:, None, :]
    response = (wet * jnp.tanh(ocean_state + ocean_import)).astype(jnp.bfloat16)
    near = response
    for axis in ("atm", "ocn"):
        low, high = shift(near, axis, 1), shift(near, axis, -1)
        near = jnp.stack([low, near, high], axis=0)
    near = jnp.swapaxes(near, 0, 1).reshape(9 * ocean_count, fields, cells)
    atm_import = backward(
        n_atmos, n_ocean, near, back_blocks, back_src_dev[:, 0], back_src_tile, back_dst_tile, atmos_count
    )
    return (ocean_import, atm_import)


def solution(mesh):
    part = ("atm", "ocn")
    three, two, one = P(part, None, None), P(part, None), P(part)
    in_specs = (three, three, one, two, one, three, two, three, two, one, one)
    return jax.shard_map(shards, mesh=mesh, in_specs=in_specs, out_specs=(three, three), check_vma=False)
```

time: 60.1 us -> 47.6 us (0.79)
  Pallas kernels: 0 us -> 13.9 us
  waiting for transfers between devices: 28.5 us -> 18.2 us
  matrix products: 10.2 us -> 0 us
  local copies, waits for them, and re-layouts: 5.05 us -> 0.16 us
  starting transfers between devices: 14.1 us -> 13.4 us
    pallas_call x0 -> x2, Pallas kernels: none -> 13.9 us  [the longest x1 7.63 us: forward(): pl.pallas_call(functools.partial(fwd_kernel, n_atmos, n_ocean), out_shape...]
    ppermute x8, waiting for transfers between devices: 28.5 us -> 18.2 us  [shift(): lax.ppermute(block, axis, [(i, (i + step) % count) for i in range(count)])]
    dot_general x4 -> x0, matrix products: 10.2 us -> none  [the longest x1 3.78 us: shards(): jnp.einsum('bfi,bij->bfj', sources, fwd_blocks, preferred_element_type=jn...]
    unnamed x18 -> x14, local copies, waits for them, and re-layouts: 3.14 us -> 0.03 us
    gather x2 -> x0, local copies, waits for them, and re-layouts: 1.8 us -> none  [the longest x1 0.9 us: shards(): nearby.reshape(9 * ocean_count, fields, cells)]
    select_n x2 -> x0, other arithmetic: 0.78 us -> none  [the longest x1 0.75 us: shards(): sources = atm_fields[fwd_src_tile]]
    ppermute x8, starting transfers between devices: 14.1 us -> 13.4 us  [shift(): lax.ppermute(block, axis, [(i, (i + step) % count) for i in range(count)])]
    convert_element_type x0 -> x1, other arithmetic: none -> 0.68 us  [shards(): response = (wet * jnp.tanh(ocean_state + ocean_import)).astype(jnp.bfloat16)]
  transfers between devices with their start and end apart: 8 -> 8, of which waited for: 7 -> 7; matrix products, arithmetic and copies ran while one was open for 1% -> 0% of each run, Pallas kernels for 0% -> 0%
where the time goes in v1:
time: 47.6 us; the launch traced here: 47.4 us
  waiting for transfers between devices  18.2 us (38%)
  Pallas kernels  13.9 us (29%)
  starting transfers between devices  13.4 us (28%)
  other arithmetic  0.98 us (2%)
  between operations  0.8 us (2%)
    ppermute x8, waiting for transfers between devices, shift(): lax.ppermute(block, axis, [(i, (i + step) % count) for i in range(count)])  18.2 us
    ppermute x8, starting transfers between devices, shift(): lax.ppermute(block, axis, [(i, (i + step) % count) for i in range(count)])  13.4 us
    pallas_call x1, Pallas kernels, forward(): pl.pallas_call(functools.partial(fwd_kernel, n_atmos, n_ocean), out_shape...  7.63 us
    pallas_call x1, Pallas kernels, backward(): pl.pallas_call(functools.partial(bwd_kernel, n_atmos, n_ocean), out_shape...  6.25 us
  transfers between devices with their start and end apart: 8, of which 7 were waited for; matrix products, arithmetic and copies ran while one was open for 0% of the time, Pallas kernels for 0%

profile of v1, /device:TPU:1, one launch (start us, length us, event | category | flops | bytes accessed | tf_op | source)
XLA Modules:
  0.0 47.4 jit_solution(2634315156392098082)
XLA Ops:
  0.7 0.0 slice-start
  0.7 7.6 %forward_blocks.1 = f32[72,24,128]{2,1,0:T(8,128)S(1)} custom-call(bf16[128,24,128]{2,1,0:T(8,128)(2,1)} %fields_hbm.1, bf16[192,128,128]{2,1,0:T(8,128)(2,1)} %blocks_hbm.1, s32[192]{0:T(256)} %src_hbm.2, s32[192]{0:T(256)} %bitcast.45, s32[192]{0:T(256)} %tile_hbm.1), custom_call_target="tpu_custom_call" | custom-call | tf_op jit(solution)/shard_map/forward_blocks/pallas_call | solution.py:118
  8.3 0.2 fusion.8
  8.5 0.1 slice_bitcast_fusion.2
  8.6 0.1 collective-permute-start
  8.6 2.6 %collective-permute-start.1 = (f16[3,8,24,128]{3,2,1,0:T(8,128)(2,1)S(1)}, f16[3,8,24,128]{3,2,1,0:T(8,128)(2,1)S(1)}, u32[]{:S(2)}, u32[]{:S(2)}) collective-permute-start(f16[3,8,24,128]{3,2,1,0:T(8,128)(2,1)S(1)} %get-tuple-element.9), channel_id=1, source_target_pairs={{0,1},{1,2},{2,3},{3,0},{4,5},{5,6},{6,7},{7,4},{8,9},{9,10},{10,1... | collective-permute-start | bytes 442376 | tf_op jit(solution)/shard_map/ppermute | solution.py:160
  11.3 3.8 %collective-permute-done = f16[3,8,24,128]{3,2,1,0:T(8,128)(2,1)S(1)} collective-permute-done((f16[3,8,24,128]{3,2,1,0:T(8,128)(2,1)S(1)}, f16[3,8,24,128]{3,2,1,0:T(8,128)(2,1)S(1)}, u32[]{:S(2)}, u32[]{:S(2)}) %collective-permute-start) | collective-permute-done | bytes 147488 | tf_op jit(solution)/shard_map/ppermute | solution.py:160
  15.0 0.0 collective-permute-done.1
  15.0 0.1 fusion.6
  15.2 4.3 %collective-permute-start.2 = (f16[8,24,128]{2,1,0:T(8,128)(2,1)S(1)}, f16[8,24,128]{2,1,0:T(8,128)(2,1)S(1)}, u32[]{:S(2)}, u32[]{:S(2)}) collective-permute-start(f16[8,24,128]{2,1,0:T(8,128)(2,1)S(1)} %get-tuple-element.12), channel_id=1, source_target_pairs={{0,28},{4,0},{8,4},{12,8},{16,12},{20,16},{24,20},{28,24},{1,29},{... | collective-permute-start | bytes 147464 | tf_op jit(solution)/shard_map/ppermute | solution.py:160
  19.5 0.0 collective-permute-start.3
  19.5 1.2 %collective-permute-done.2 = f16[8,24,128]{2,1,0:T(8,128)(2,1)S(1)} collective-permute-done((f16[8,24,128]{2,1,0:T(8,128)(2,1)S(1)}, f16[8,24,128]{2,1,0:T(8,128)(2,1)S(1)}, u32[]{:S(2)}, u32[]{:S(2)}) %collective-permute-start.2) | collective-permute-done | bytes 49184 | tf_op jit(solution)/shard_map/ppermute | solution.py:160
  20.7 4.5 %collective-permute-done.3 = f16[8,24,128]{2,1,0:T(8,128)(2,1)S(1)} collective-permute-done((f16[8,24,128]{2,1,0:T(8,128)(2,1)S(1)}, f16[8,24,128]{2,1,0:T(8,128)(2,1)S(1)}, u32[]{:S(2)}, u32[]{:S(2)}) %collective-permute-start.3) | collective-permute-done | bytes 49184 | tf_op jit(solution)/shard_map/ppermute | solution.py:160
  25.1 0.7 %multiply_convert_fusion = (bf16[8,24,128]{2,1,0:T(8,128)(2,1)S(1)}, f32[8,24,128]{2,1,0:T(8,128)}) fusion(f32[8,24,128]{2,1,0:T(8,128)S(1)} %copy-done.3, f32[8,128]{1,0:T(8,128)S(1)} %convert_element_type.42, f16[8,24,128]{2,1,0:T(8,128)(2,1)S(1)} %collective-permute-done.3, f16[8,24,128]{2,1,0:T(8,128)(2,1)S(1)} %collective-permute-done.2, ...), kind=kLoop, calls=%fused_computation.10 | loop fusion | flops 172032 | bytes 446464 | tf_op jit(solution)/shard_map/convert_element_type | solution.py:187
  25.8 0.1 collective-permute-start.5
  25.9 1.4 %collective-permute-start.4 = (bf16[8,24,128]{2,1,0:T(8,128)(2,1)S(1)}, bf16[8,24,128]{2,1,0:T(8,128)(2,1)S(1)}, u32[]{:S(2)}, u32[]{:S(2)}) collective-permute-start(bf16[8,24,128]{2,1,0:T(8,128)(2,1)S(1)} %get-tuple-element.2), channel_id=1, source_target_pairs={{0,4},{4,8},{8,12},{12,16},{16,20},{20,24},{24,28},{28,0},{1,5},{5... | collective-permute-start | bytes 147464 | tf_op jit(solution)/shard_map/ppermute | solution.py:160
  27.3 1.5 %collective-permute-done.5 = bf16[8,24,128]{2,1,0:T(8,128)(2,1)S(1)} collective-permute-done((bf16[8,24,128]{2,1,0:T(8,128)(2,1)S(1)}, bf16[8,24,128]{2,1,0:T(8,128)(2,1)S(1)}, u32[]{:S(2)}, u32[]{:S(2)}) %collective-permute-start.5) | collective-permute-done | bytes 49184 | tf_op jit(solution)/shard_map/ppermute | solution.py:160
  28.8 2.8 %collective-permute-done.4 = bf16[8,24,128]{2,1,0:T(8,128)(2,1)S(1)} collective-permute-done((bf16[8,24,128]{2,1,0:T(8,128)(2,1)S(1)}, bf16[8,24,128]{2,1,0:T(8,128)(2,1)S(1)}, u32[]{:S(2)}, u32[]{:S(2)}) %collective-permute-start.4) | collective-permute-done | bytes 49184 | tf_op jit(solution)/shard_map/ppermute | solution.py:160
  31.6 4.9 %collective-permute-start.6 = (bf16[3,8,24,128]{3,2,1,0:T(8,128)(2,1)S(1)}, bf16[3,8,24,128]{3,2,1,0:T(8,128)(2,1)S(1)}, u32[]{:S(2)}, u32[]{:S(2)}) collective-permute-start(bf16[3,8,24,128]{3,2,1,0:T(8,128)(2,1)S(1)} %get-tuple-element.11), channel_id=1, source_target_pairs={{0,1},{1,2},{2,3},{3,0},{4,5},{5,6},{6,7},{7,4},{8,9},{9,10},{10,1... | collective-permute-start | bytes 442376 | tf_op jit(solution)/shard_map/ppermute | solution.py:160
  36.4 0.0 collective-permute-start.7
  36.4 2.8 %collective-permute-done.6 = bf16[3,8,24,128]{3,2,1,0:T(8,128)(2,1)S(1)} collective-permute-done((bf16[3,8,24,128]{3,2,1,0:T(8,128)(2,1)S(1)}, bf16[3,8,24,128]{3,2,1,0:T(8,128)(2,1)S(1)}, u32[]{:S(2)}, u32[]{:S(2)}) %collective-permute-start.6) | collective-permute-done | bytes 147488 | tf_op jit(solution)/shard_map/ppermute | solution.py:160
  39.2 1.8 %collective-permute-done.7 = bf16[3,8,24,128]{3,2,1,0:T(8,128)(2,1)S(1)} collective-permute-done((bf16[3,8,24,128]{3,2,1,0:T(8,128)(2,1)S(1)}, bf16[3,8,24,128]{3,2,1,0:T(8,128)(2,1)S(1)}, u32[]{:S(2)}, u32[]{:S(2)}) %collective-permute-start.7) | collective-permute-done | bytes 147488 | tf_op jit(solution)/shard_map/ppermute | solution.py:160
  41.0 0.1 maximum_bitcast_fusion
  41.2 6.3 %backward_blocks.1 = f32[128,24,128]{2,1,0:T(8,128)} custom-call(bf16[72,24,128]{2,1,0:T(8,128)(2,1)S(1)} %bitcast.38, bf16[192,128,128]{2,1,0:T(8,128)(2,1)S(1)} %bitcast.36, s32[192]{0:T(256)S(1)} %bitcast.39, s32[192]{0:T(256)S(1)} %copy-done.1, s32[192]{0:T(256)S(1)} %copy-done.2), custom_call_target="tpu_custom_call" | custom-call | tf_op jit(solution)/shard_map/backward_blocks/pallas_call | solution.py:141
  (18 shorter events, 0.1 us)
Async XLA Ops:
  0.6 18.9 %copy-start.4 = (s32[8,128]{1,0:T(8,128)S(1)}, s32[8,128]{1,0:T(8,128)}, u32[]{:S(2)}) copy-start(s32[8,128]{1,0:T(8,128)} %param.17) | copy-start | bytes 12292
  0.6 24.5 %copy-start.3 = (f32[8,24,128]{2,1,0:T(8,128)S(1)}, f32[8,24,128]{2,1,0:T(8,128)}, u32[]{:S(2)}) copy-start(f32[8,24,128]{2,1,0:T(8,128)} %param.16) | copy-start | bytes 294916
  0.7 40.5 %slice-start = ((s8[6291456]{0:T(1024)(128)(4,1)}), s8[4194304]{0:T(1024)(128)(4,1)S(1)}, s32[]{:S(2)}) async-start(s8[6291456]{0:T(1024)(128)(4,1)} %bitcast.35), calls=%async_computation | async-start | bytes 8388608
  0.7 40.5 %slice-start.1 = ((s8[6291456]{0:T(1024)(128)(4,1)}), s8[2097152]{0:T(1024)(128)(4,1)S(1)}, s32[]{:S(2)}) async-start(s8[6291456]{0:T(1024)(128)(4,1)} %bitcast.35), calls=%async_computation.1 | async-start | bytes 4194304
  0.7 40.5 %copy-start = (s32[192,1]{0,1:T(1,128)S(1)}, s32[192,1]{0,1:T(1,128)}, u32[]{:S(2)}) copy-start(s32[192,1]{0,1:T(1,128)} %param.19) | copy-start | bytes 2308
  0.7 40.5 %copy-start.1 = (s32[192]{0:T(256)S(1)}, s32[192]{0:T(256)}, u32[]{:S(2)}) copy-start(s32[192]{0:T(256)} %src_hbm.3) | copy-start | bytes 2308
  0.7 40.5 %copy-start.2 = (s32[192]{0:T(256)S(1)}, s32[192]{0:T(256)}, u32[]{:S(2)}) copy-start(s32[192]{0:T(256)} %dst_hbm.1) | copy-start | bytes 2308
  8.6 6.5 %collective-permute-start = (f16[3,8,24,128]{3,2,1,0:T(8,128)(2,1)S(1)}, f16[3,8,24,128]{3,2,1,0:T(8,128)(2,1)S(1)}, u32[]{:S(2)}, u32[]{:S(2)}) collective-permute-start(f16[3,8,24,128]{3,2,1,0:T(8,128)(2,1)S(1)} %get-tuple-element.8), channel_id=1, source_target_pairs={{0,3},{1,0},{2,1},{3,2},{4,7},{5,4},{6,5},{7,6},{8,11},{9,8},{10,9... | collective-permute-start | bytes 442376 | tf_op jit(solution)/shard_map/ppermute | solution.py:160
  8.6 6.4 %collective-permute-start.1 = (f16[3,8,24,128]{3,2,1,0:T(8,128)(2,1)S(1)}, f16[3,8,24,128]{3,2,1,0:T(8,128)(2,1)S(1)}, u32[]{:S(2)}, u32[]{:S(2)}) collective-permute-start(f16[3,8,24,128]{3,2,1,0:T(8,128)(2,1)S(1)} %get-tuple-element.9), channel_id=1, source_target_pairs={{0,1},{1,2},{2,3},{3,0},{4,5},{5,6},{6,7},{7,4},{8,9},{9,10},{10,1... | collective-permute-start | bytes 442376 | tf_op jit(solution)/shard_map/ppermute | solution.py:160
  15.2 5.5 %collective-permute-start.2 = (f16[8,24,128]{2,1,0:T(8,128)(2,1)S(1)}, f16[8,24,128]{2,1,0:T(8,128)(2,1)S(1)}, u32[]{:S(2)}, u32[]{:S(2)}) collective-permute-start(f16[8,24,128]{2,1,0:T(8,128)(2,1)S(1)} %get-tuple-element.12), channel_id=1, source_target_pairs={{0,28},{4,0},{8,4},{12,8},{16,12},{20,16},{24,20},{28,24},{1,29},{... | collective-permute-start | bytes 147464 | tf_op jit(solution)/shard_map/ppermute | solution.py:160
  19.5 5.6 %collective-permute-start.3 = (f16[8,24,128]{2,1,0:T(8,128)(2,1)S(1)}, f16[8,24,128]{2,1,0:T(8,128)(2,1)S(1)}, u32[]{:S(2)}, u32[]{:S(2)}) collective-permute-start(f16[8,24,128]{2,1,0:T(8,128)(2,1)S(1)} %get-tuple-element.13), channel_id=1, source_target_pairs={{0,4},{4,8},{8,12},{12,16},{16,20},{20,24},{24,28},{28,0},{1,5},{5... | collective-permute-start | bytes 147464 | tf_op jit(solution)/shard_map/ppermute | solution.py:160
  25.8 2.9 %collective-permute-start.5 = (bf16[8,24,128]{2,1,0:T(8,128)(2,1)S(1)}, bf16[8,24,128]{2,1,0:T(8,128)(2,1)S(1)}, u32[]{:S(2)}, u32[]{:S(2)}) collective-permute-start(bf16[8,24,128]{2,1,0:T(8,128)(2,1)S(1)} %get-tuple-element.2), channel_id=1, source_target_pairs={{0,28},{4,0},{8,4},{12,8},{16,12},{20,16},{24,20},{28,24},{1,29},{... | collective-permute-start | bytes 147464 | tf_op jit(solution)/shard_map/ppermute | solution.py:160
  25.9 5.6 %collective-permute-start.4 = (bf16[8,24,128]{2,1,0:T(8,128)(2,1)S(1)}, bf16[8,24,128]{2,1,0:T(8,128)(2,1)S(1)}, u32[]{:S(2)}, u32[]{:S(2)}) collective-permute-start(bf16[8,24,128]{2,1,0:T(8,128)(2,1)S(1)} %get-tuple-element.2), channel_id=1, source_target_pairs={{0,4},{4,8},{8,12},{12,16},{16,20},{20,24},{24,28},{28,0},{1,5},{5... | collective-permute-start | bytes 147464 | tf_op jit(solution)/shard_map/ppermute | solution.py:160
  31.6 7.7 %collective-permute-start.6 = (bf16[3,8,24,128]{3,2,1,0:T(8,128)(2,1)S(1)}, bf16[3,8,24,128]{3,2,1,0:T(8,128)(2,1)S(1)}, u32[]{:S(2)}, u32[]{:S(2)}) collective-permute-start(bf16[3,8,24,128]{3,2,1,0:T(8,128)(2,1)S(1)} %get-tuple-element.11), channel_id=1, source_target_pairs={{0,1},{1,2},{2,3},{3,0},{4,5},{5,6},{6,7},{7,4},{8,9},{9,10},{10,1... | collective-permute-start | bytes 442376 | tf_op jit(solution)/shard_map/ppermute | solution.py:160
  36.4 4.6 %collective-permute-start.7 = (bf16[3,8,24,128]{3,2,1,0:T(8,128)(2,1)S(1)}, bf16[3,8,24,128]{3,2,1,0:T(8,128)(2,1)S(1)}, u32[]{:S(2)}, u32[]{:S(2)}) collective-permute-start(bf16[3,8,24,128]{3,2,1,0:T(8,128)(2,1)S(1)} %get-tuple-element.11), channel_id=1, source_target_pairs={{0,3},{1,0},{2,1},{3,2},{4,7},{5,4},{6,5},{7,6},{8,11},{9,8},{10,9... | collective-permute-start | bytes 442376 | tf_op jit(solution)/shard_map/ppermute | solution.py:160

commit v2 on v1

v2 whole, which is shorter than its diff:
```python
import functools

import jax
import jax.numpy as jnp
from jax import lax
from jax.experimental import pallas as pl
from jax.experimental.pallas import tpu as pltpu
from jax.sharding import PartitionSpec as P


CHUNKS = 4
UNROLL = 48
GROUP = 4
F32 = jnp.float32
F16 = jnp.float16
FIRST_SCALE = 8.0
SECOND_SCALE = 2.0


def neighbour_ids(n_atmos, n_ocean):
    row, col = lax.axis_index("atm"), lax.axis_index("ocn")
    rows = [lax.rem(row + step + n_atmos, n_atmos) for step in (-1, 0, 1)]
    cols = [lax.rem(col + step + n_ocean, n_ocean) for step in (-1, 0, 1)]
    return [r * n_ocean + c for r in rows for c in cols]


def fill_table(table, n_atmos, n_ocean):
    for place, device in enumerate(neighbour_ids(n_atmos, n_ocean)):
        table[device] = place


def stacked(first, second):
    spare = jnp.zeros((-first.shape[0] % 16, first.shape[1]), first.dtype)
    first = jnp.concatenate([first, spare], axis=0)
    second = jnp.concatenate([second, spare], axis=0)
    empty = jnp.zeros_like(first)
    return jnp.concatenate(
        [jnp.concatenate([first, empty], axis=1), jnp.concatenate([empty, second], axis=1)], axis=0
    )


def add_group(total, targets, products):
    sums = []
    for k, target in enumerate(targets):
        value = products[k]
        for j in range(k):
            value = value + jnp.where(targets[j] == target, products[j], 0.0)
        sums.append(total[target] + value)
    for target, value in zip(targets, sums):
        total[target] = value


def block_sums(blocks, source_of, target_of, load, total, begin, end):
    rows, cells = total.shape[1:]
    pairs = blocks.reshape(blocks.shape[0] // 2, 2 * cells, cells)

    def run(first, carry):
        at = first * UNROLL
        for group in range(0, UNROLL, GROUP):
            products = []
            for step in range(group, group + GROUP, 2):
                sources = stacked(load(source_of(at + step)), load(source_of(at + step + 1)))
                product = jnp.dot(sources, pairs[(at + step) // 2], preferred_element_type=F32)
                half = product.shape[0] // 2
                products += [product[:rows], product[half : half + rows]]
            add_group(total, [target_of(at + step) for step in range(group, group + GROUP)], products)
        return carry

    lax.fori_loop(begin // UNROLL, end // UNROLL, run, 0)


def start_all(copies):
    for copy in copies:
        copy.start()
    return copies


def fwd_kernel(
    n_atmos, n_ocean, fields_hbm, blocks_hbm, src_hbm, dev_hbm, tile_hbm, state_hbm, mask_hbm,
    own, low, high, surface, blocks, fields, total, mask, src, dev, tile, table, sems, index_sems,
):
    tiles = own.shape[1]
    rows = fields.shape[1]
    small = start_all([
        pltpu.make_async_copy(src_hbm, src, index_sems.at[0]),
        pltpu.make_async_copy(dev_hbm, dev, index_sems.at[1]),
        pltpu.make_async_copy(tile_hbm, tile, index_sems.at[2]),
        pltpu.make_async_copy(fields_hbm, fields, index_sems.at[3]),
    ])
    count = blocks.shape[0] // CHUNKS
    weights = start_all([
        pltpu.make_async_copy(
            blocks_hbm.at[pl.ds(c * count, count)], blocks.at[pl.ds(c * count, count)], sems.at[c]
        )
        for c in range(CHUNKS)
    ])
    late = start_all([
        pltpu.make_async_copy(state_hbm, surface.at[:, pl.ds(0, rows), :], index_sems.at[4]),
        pltpu.make_async_copy(mask_hbm, mask, index_sems.at[5]),
    ])
    fill_table(table, n_atmos, n_ocean)
    total[...] = jnp.zeros_like(total)
    for copy in small:
        copy.wait()
    for c in range(CHUNKS):
        weights[c].wait()
        block_sums(
            blocks, lambda b: src[b], lambda b: table[dev[b]] * tiles + tile[b],
            lambda s: fields[s], total, c * count, (c + 1) * count,
        )
    for row in range(3):
        for col, out in enumerate((low, own, high)):
            first = (row * 3 + col) * tiles
            part = total[first : first + tiles]
            out[row] = part
    for copy in late:
        copy.wait()
    wet = mask[...].astype(F32)
    surface[:, rows:, :] = jnp.broadcast_to(wet[:, None, :], (tiles, surface.shape[1] - rows, wet.shape[1]))


def bwd_kernel(n_atmos, n_ocean, near_ref, blocks, dev_hbm, src_hbm, dst_hbm, total, dev, src, dst, table, index_sems):
    tiles = near_ref.shape[0] // 9
    small = start_all([
        pltpu.make_async_copy(src_hbm, src, index_sems.at[0]),
        pltpu.make_async_copy(dev_hbm, dev, index_sems.at[1]),
        pltpu.make_async_copy(dst_hbm, dst, index_sems.at[2]),
    ])
    fill_table(table, n_atmos, n_ocean)
    total[...] = jnp.zeros_like(total)
    for copy in small:
        copy.wait()
    block_sums(
        blocks, lambda b: table[dev[b]] * tiles + src[b], lambda b: dst[b],
        lambda s: near_ref[s], total, 0, blocks.shape[0],
    )


def in_hbm(*arrays):
    return [pltpu.with_memory_space_constraint(a, pltpu.HBM) for a in arrays]


def hbm():
    return pl.BlockSpec(memory_space=pl.ANY)


def vmem():
    return pl.BlockSpec(memory_space=pltpu.VMEM)


def forward(n_atmos, n_ocean, atm_fields, fwd_blocks, src, dev, tile, state, mask):
    fields, cells = atm_fields.shape[1:]
    count = fwd_blocks.shape[0]
    tiles = state.shape[0]
    index = pltpu.SMEM((count,), jnp.int32)
    part = (3, tiles, fields, cells)
    return pl.pallas_call(
        functools.partial(fwd_kernel, n_atmos, n_ocean),
        out_shape=[
            jax.ShapeDtypeStruct(part, F32),
            jax.ShapeDtypeStruct(part, F32),
            jax.ShapeDtypeStruct(part, F32),
            jax.ShapeDtypeStruct((tiles, fields + 8, cells), F32),
        ],
        in_specs=[hbm()] * 7,
        out_specs=[vmem()] * 4,
        scratch_shapes=[
            pltpu.VMEM(fwd_blocks.shape, fwd_blocks.dtype),
            pltpu.VMEM(atm_fields.shape, atm_fields.dtype),
            pltpu.VMEM((9 * tiles, fields, cells), F32),
            pltpu.VMEM(mask.shape, mask.dtype),
            index, index, index,
            pltpu.SMEM((n_atmos * n_ocean,), jnp.int32),
            pltpu.SemaphoreType.DMA((CHUNKS,)),
            pltpu.SemaphoreType.DMA((6,)),
        ],
        compiler_params=pltpu.CompilerParams(vmem_limit_bytes=16 * 2**20),
        name="forward_blocks",
    )(*in_hbm(atm_fields, fwd_blocks, src, dev, tile, state, mask))


def backward(n_atmos, n_ocean, near, back_blocks, dev, src, dst, atmos_count):
    fields, cells = near.shape[1:]
    count = back_blocks.shape[0]
    index = pltpu.SMEM((count,), jnp.int32)
    return pl.pallas_call(
        functools.partial(bwd_kernel, n_atmos, n_ocean),
        out_shape=jax.ShapeDtypeStruct((atmos_count, fields, cells), F32),
        in_specs=[vmem()] * 2 + [hbm()] * 3,
        out_specs=vmem(),
        scratch_shapes=[
            index, index, index,
            pltpu.SMEM((n_atmos * n_ocean,), jnp.int32),
            pltpu.SemaphoreType.DMA((3,)),
        ],
        compiler_params=pltpu.CompilerParams(vmem_limit_bytes=16 * 2**20),
        name="backward_blocks",
    )(near, back_blocks, dev, src, dst)


def shift(block, axis, step):
    count = lax.axis_size(axis)
    return lax.ppermute(block, axis, [(i, (i + step) % count) for i in range(count)])


def swap(low, high, axis, step=1):
    from_upper = shift(low, axis, -step)
    from_lower = shift(high, axis, step)
    return from_upper, from_lower


def shards(
    atm_fields, fwd_blocks, fwd_src_tile, fwd_dst_dev, fwd_dst_tile, ocean_state, wet_mask,
    back_blocks, back_src_dev, back_src_tile, back_dst_tile,
):
    n_atmos = lax.axis_size("atm")
    n_ocean = lax.axis_size("ocn")
    fields, cells = atm_fields.shape[1:]
    ocean_count = ocean_state.shape[0]
    atmos_count = atm_fields.shape[0]
    own, low, high, surface = forward(
        n_atmos, n_ocean, atm_fields, fwd_blocks, fwd_src_tile, fwd_dst_dev[:, 0], fwd_dst_tile, ocean_state, wet_mask
    )
    upper, lower = swap((low * FIRST_SCALE).astype(F16), (high * FIRST_SCALE).astype(F16), "ocn")
    above, below = swap(surface, surface, "atm")
    surface = jnp.stack([below, surface, above])
    row_sums = own + (upper.astype(F32) + lower.astype(F32)) * (1.0 / FIRST_SCALE)
    sent = (row_sums * SECOND_SCALE).astype(F16)
    from_above, from_below = swap(sent[:2], sent[1:], "atm")
    from_two_above, from_two_below = swap(sent[0], sent[2], "atm", 2)
    near_sums = jnp.stack([from_below[0], from_below[1], from_above[1]]).astype(F32)
    far_sums = jnp.stack([from_two_below, from_above[0], from_two_above]).astype(F32)
    sums = row_sums + (near_sums + far_sums) * (1.0 / SECOND_SCALE)
    wet = surface[:, :, fields : fields + 1]
    response = (wet * jnp.tanh(surface[:, :, :fields] + sums)).astype(jnp.bfloat16)
    upper, lower = swap(response, response, "ocn")
    near = jnp.stack([lower, response, upper], axis=1).reshape(9 * ocean_count, fields, cells)
    atm_import = backward(
        n_atmos, n_ocean, near, back_blocks, back_src_dev[:, 0], back_src_tile, back_dst_tile, atmos_count
    )
    return (sums[1], atm_import)


def solution(mesh):
    part = ("atm", "ocn")
    three, two, one = P(part, None, None), P(part, None), P(part)
    in_specs = (three, three, one, two, one, three, two, three, two, one, one)
    return jax.shard_map(shards, mesh=mesh, in_specs=in_specs, out_specs=(three, three), check_vma=False)
```

time: 47.6 us -> 42.3 us (0.89); the launches traced: 47.4 us -> 41.5 us
  Pallas kernels: 13.9 us -> 7.38 us
  starting transfers between devices: 13.4 us -> 16.9 us
  waiting for transfers between devices: 18.2 us -> 15.3 us
  local copies, waits for them, and re-layouts: 0.16 us -> 0.79 us
  other arithmetic: 0.98 us -> 0.39 us
    pallas_call x1, Pallas kernels: 7.63 us -> 3.79 us  [forward(): pl.pallas_call(functools.partial(fwd_kernel, n_atmos, n_ocean), out_shape...]
    ppermute x8 -> x10, starting transfers between devices: 13.4 us -> 16.9 us  [shift(): lax.ppermute(block, axis, [(i, (i + step) % count) for i in range(count)])]
    ppermute x8 -> x10, waiting for transfers between devices: 18.2 us -> 15.3 us  [shift(): lax.ppermute(block, axis, [(i, (i + step) % count) for i in range(count)])]
    pallas_call x1, Pallas kernels: 6.25 us -> 3.6 us  [backward(): pl.pallas_call(functools.partial(bwd_kernel, n_atmos, n_ocean), out_shape...]
    squeeze x0 -> x2, local copies, waits for them, and re-layouts: none -> 0.67 us  [the longest x1 0.65 us: shards(): return (sums[1], atm_import)]
  transfers between devices with their start and end apart: 8 -> 10, of which waited for: 7 -> 5; matrix products, arithmetic and copies ran while one was open for 0% -> 2% of each run, Pallas kernels for 0% -> 0%
where the time goes in v2:
time: 42.3 us; the launch traced here: 41.5 us
  starting transfers between devices  16.9 us (40%)
  waiting for transfers between devices  15.3 us (36%)
  Pallas kernels  7.38 us (17%)
  between operations  0.81 us (2%)
  local copies, waits for them, and re-layouts  0.79 us (2%)
    ppermute x10, starting transfers between devices, shift(): lax.ppermute(block, axis, [(i, (i + step) % count) for i in range(count)])  16.9 us
    ppermute x10, waiting for transfers between devices, shift(): lax.ppermute(block, axis, [(i, (i + step) % count) for i in range(count)])  15.3 us
    pallas_call x1, Pallas kernels, forward(): pl.pallas_call(functools.partial(fwd_kernel, n_atmos, n_ocean), out_shape...  3.79 us
    pallas_call x1, Pallas kernels, backward(): pl.pallas_call(functools.partial(bwd_kernel, n_atmos, n_ocean), out_shape...  3.6 us
  transfers between devices with their start and end apart: 10, of which 5 were waited for; matrix products, arithmetic and copies ran while one was open for 2% of the time, Pallas kernels for 0%

profile of v2, /device:TPU:1, one launch (start us, length us, event | category | flops | bytes accessed | tf_op | source)
XLA Modules:
  0.0 41.5 jit_solution(3129962323682063699)
XLA Ops:
  0.6 0.0 slice-start.1
  0.7 3.8 %forward_blocks.1 = (f32[3,8,24,128]{3,2,1,0:T(8,128)S(1)}, f32[3,8,24,128]{3,2,1,0:T(8,128)S(1)}, f32[3,8,24,128]{3,2,1,0:T(8,128)S(1)}, f32[8,32,128]{2,1,0:T(8,128)S(1)}) custom-call(bf16[128,24,128]{2,1,0:T(8,128)(2,1)} %fields_hbm.1, bf16[192,128,128]{2,1,0:T(8,128)(2,1)} %blocks_hbm.1, s32[192]{0:T(256)} %src_hbm.2, s32[192]{0:T(256)} %bitcast.34, ...), custom_call_target="tpu_custom_call" | custom-call | tf_op jit(solution)/shard_map/forward_blocks/pallas_call | solution.py:157
  4.5 5.1 %collective-permute-start.7 = (f32[8,32,128]{2,1,0:T(8,128)S(1)}, f32[8,32,128]{2,1,0:T(8,128)S(1)}, u32[]{:S(2)}, u32[]{:S(2)}) collective-permute-start(f32[8,32,128]{2,1,0:T(8,128)S(1)} %get-tuple-element.9), channel_id=1, source_target_pairs={{0,28},{4,0},{8,4},{12,8},{16,12},{20,16},{24,20},{28,24},{1,29},{... | collective-permute-start | bytes 393224 | tf_op jit(solution)/shard_map/ppermute | solution.py:203
  9.7 2.1 %collective-permute-start.1 = (f16[3,8,24,128]{3,2,1,0:T(8,128)(2,1)S(1)}, f16[3,8,24,128]{3,2,1,0:T(8,128)(2,1)S(1)}, u32[]{:S(2)}, u32[]{:S(2)}) collective-permute-start(f16[3,8,24,128]{3,2,1,0:T(8,128)(2,1)S(1)} %multiply_convert_fusion.1), channel_id=1, source_target_pairs={{0,1},{1,2},{2,3},{3,0},{4,5},{5,6},{6,7},{7,4},{8,9},{9,10},{10,1... | collective-permute-start | bytes 442376 | tf_op jit(solution)/shard_map/ppermute | solution.py:203
  11.8 0.1 collective-permute-start
  11.9 0.0 collective-permute-done.7
  11.9 4.3 %collective-permute-done.6 = f32[8,32,128]{2,1,0:T(8,128)S(1)} collective-permute-done((f32[8,32,128]{2,1,0:T(8,128)S(1)}, f32[8,32,128]{2,1,0:T(8,128)S(1)}, u32[]{:S(2)}, u32[]{:S(2)}) %collective-permute-start.6) | collective-permute-done | bytes 131104 | tf_op jit(solution)/shard_map/ppermute | solution.py:203
  16.2 0.5 %collective-permute-done = f16[3,8,24,128]{3,2,1,0:T(8,128)(2,1)S(1)} collective-permute-done((f16[3,8,24,128]{3,2,1,0:T(8,128)(2,1)S(1)}, f16[3,8,24,128]{3,2,1,0:T(8,128)(2,1)S(1)}, u32[]{:S(2)}, u32[]{:S(2)}) %collective-permute-start) | collective-permute-done | bytes 147488 | tf_op jit(solution)/shard_map/ppermute | solution.py:203
  16.7 0.1 multiply_convert_fusion
  16.8 4.2 %collective-permute-start.3 = (f16[2,8,24,128]{3,2,1,0:T(8,128)(2,1)S(1)}, f16[2,8,24,128]{3,2,1,0:T(8,128)(2,1)S(1)}, u32[]{:S(2)}, u32[]{:S(2)}) collective-permute-start(f16[2,8,24,128]{3,2,1,0:T(8,128)(2,1)S(1)} %get-tuple-element.13), channel_id=1, source_target_pairs={{0,28},{4,0},{8,4},{12,8},{16,12},{20,16},{24,20},{28,24},{1,29},{... | collective-permute-start | bytes 294920 | tf_op jit(solution)/shard_map/ppermute | solution.py:203
  21.1 0.1 collective-permute-start.4
  21.1 3.3 %collective-permute-start.5 = (f16[8,24,128]{2,1,0:T(8,128)(2,1)S(1)}, f16[8,24,128]{2,1,0:T(8,128)(2,1)S(1)}, u32[]{:S(2)}, u32[]{:S(2)}) collective-permute-start(f16[8,24,128]{2,1,0:T(8,128)(2,1)S(1)} %get-tuple-element.15), channel_id=1, source_target_pairs={{0,24},{4,28},{8,0},{12,4},{16,8},{20,12},{24,16},{28,20},{1,25},{... | collective-permute-start | bytes 147464 | tf_op jit(solution)/shard_map/ppermute | solution.py:203
  24.4 0.0 collective-permute-start.2
  24.4 2.1 %collective-permute-done.4 = f16[8,24,128]{2,1,0:T(8,128)(2,1)S(1)} collective-permute-done((f16[8,24,128]{2,1,0:T(8,128)(2,1)S(1)}, f16[8,24,128]{2,1,0:T(8,128)(2,1)S(1)}, u32[]{:S(2)}, u32[]{:S(2)}) %collective-permute-start.4) | collective-permute-done | bytes 49184 | tf_op jit(solution)/shard_map/ppermute | solution.py:203
  26.5 0.0 collective-permute-done.5
  26.5 4.7 %collective-permute-done.2 = f16[2,8,24,128]{3,2,1,0:T(8,128)(2,1)S(1)} collective-permute-done((f16[2,8,24,128]{3,2,1,0:T(8,128)(2,1)S(1)}, f16[2,8,24,128]{3,2,1,0:T(8,128)(2,1)S(1)}, u32[]{:S(2)}, u32[]{:S(2)}) %collective-permute-start.2) | collective-permute-done | bytes 98336 | tf_op jit(solution)/shard_map/ppermute | solution.py:203
  31.2 0.2 fusion.3
  31.4 1.2 %collective-permute-start.9 = (bf16[3,8,24,128]{3,2,1,0:T(8,128)(2,1)S(1)}, bf16[3,8,24,128]{3,2,1,0:T(8,128)(2,1)S(1)}, u32[]{:S(2)}, u32[]{:S(2)}) collective-permute-start(bf16[3,8,24,128]{3,2,1,0:T(8,128)(2,1)S(1)} %get-tuple-element.10), channel_id=1, source_target_pairs={{0,3},{1,0},{2,1},{3,2},{4,7},{5,4},{6,5},{7,6},{8,11},{9,8},{10,9... | collective-permute-start | bytes 442376 | tf_op jit(solution)/shard_map/ppermute | solution.py:203
  32.5 0.9 %collective-permute-start.8 = (bf16[3,8,24,128]{3,2,1,0:T(8,128)(2,1)S(1)}, bf16[3,8,24,128]{3,2,1,0:T(8,128)(2,1)S(1)}, u32[]{:S(2)}, u32[]{:S(2)}) collective-permute-start(bf16[3,8,24,128]{3,2,1,0:T(8,128)(2,1)S(1)} %get-tuple-element.10), channel_id=1, source_target_pairs={{0,1},{1,2},{2,3},{3,0},{4,5},{5,6},{6,7},{7,4},{8,9},{9,10},{10,1... | collective-permute-start | bytes 442376 | tf_op jit(solution)/shard_map/ppermute | solution.py:203
  33.4 0.6 %slice_bitcast_fusion = f32[8,24,128]{2,1,0:T(8,128)} fusion(f32[3,8,24,128]{3,2,1,0:T(8,128)S(1)} %get-tuple-element.11), kind=kLoop, calls=%fused_computation.12 | loop fusion | bytes 196608 | tf_op jit(solution)/shard_map/squeeze | solution.py:241
  34.1 3.7 %collective-permute-done.9 = bf16[3,8,24,128]{3,2,1,0:T(8,128)(2,1)S(1)} collective-permute-done((bf16[3,8,24,128]{3,2,1,0:T(8,128)(2,1)S(1)}, bf16[3,8,24,128]{3,2,1,0:T(8,128)(2,1)S(1)}, u32[]{:S(2)}, u32[]{:S(2)}) %collective-permute-start.9) | collective-permute-done | bytes 147488 | tf_op jit(solution)/shard_map/ppermute | solution.py:203
  37.8 0.0 collective-permute-done.8
  37.8 0.1 pad_maximum_fusion
  37.9 3.6 %backward_blocks.1 = f32[128,24,128]{2,1,0:T(8,128)} custom-call(bf16[72,24,128]{2,1,0:T(8,128)(2,1)S(1)} %bitcast.20, bf16[192,128,128]{2,1,0:T(8,128)(2,1)S(1)} %bitcast.19, s32[192]{0:T(256)S(1)} %bitcast.23, s32[192]{0:T(256)S(1)} %copy-done.1, s32[192]{0:T(256)S(1)} %copy-done.2), custom_call_target="tpu_custom_call" | custom-call | tf_op jit(solution)/shard_map/backward_blocks/pallas_call | solution.py:186
  (20 shorter events, 0.2 us)
Async XLA Ops:
  0.6 37.2 %slice-start = ((s8[6291456]{0:T(1024)(128)(4,1)}), s8[4194304]{0:T(1024)(128)(4,1)S(1)}, s32[]{:S(2)}) async-start(s8[6291456]{0:T(1024)(128)(4,1)} %bitcast.18), calls=%async_computation | async-start | bytes 8388608
  0.6 37.2 %slice-start.1 = ((s8[6291456]{0:T(1024)(128)(4,1)}), s8[2097152]{0:T(1024)(128)(4,1)S(1)}, s32[]{:S(2)}) async-start(s8[6291456]{0:T(1024)(128)(4,1)} %bitcast.18), calls=%async_computation.1 | async-start | bytes 4194304
  0.7 37.2 %copy-start = (s32[192,1]{0,1:T(1,128)S(1)}, s32[192,1]{0,1:T(1,128)}, u32[]{:S(2)}) copy-start(s32[192,1]{0,1:T(1,128)} %param.19) | copy-start | bytes 2308
  0.7 37.2 %copy-start.1 = (s32[192]{0:T(256)S(1)}, s32[192]{0:T(256)}, u32[]{:S(2)}) copy-start(s32[192]{0:T(256)} %src_hbm.3) | copy-start | bytes 2308
  0.7 37.2 %copy-start.2 = (s32[192]{0:T(256)S(1)}, s32[192]{0:T(256)}, u32[]{:S(2)}) copy-start(s32[192]{0:T(256)} %dst_hbm.1) | copy-start | bytes 2308
  4.5 7.4 %collective-permute-start.7 = (f32[8,32,128]{2,1,0:T(8,128)S(1)}, f32[8,32,128]{2,1,0:T(8,128)S(1)}, u32[]{:S(2)}, u32[]{:S(2)}) collective-permute-start(f32[8,32,128]{2,1,0:T(8,128)S(1)} %get-tuple-element.9), channel_id=1, source_target_pairs={{0,28},{4,0},{8,4},{12,8},{16,12},{20,16},{24,20},{28,24},{1,29},{... | collective-permute-start | bytes 393224 | tf_op jit(solution)/shard_map/ppermute | solution.py:203
  9.6 6.5 %collective-permute-start.6 = (f32[8,32,128]{2,1,0:T(8,128)S(1)}, f32[8,32,128]{2,1,0:T(8,128)S(1)}, u32[]{:S(2)}, u32[]{:S(2)}) collective-permute-start(f32[8,32,128]{2,1,0:T(8,128)S(1)} %get-tuple-element.9), channel_id=1, source_target_pairs={{0,4},{4,8},{8,12},{12,16},{16,20},{20,24},{24,28},{28,0},{1,5},{5... | collective-permute-start | bytes 393224 | tf_op jit(solution)/shard_map/ppermute | solution.py:203
  9.7 6.5 %collective-permute-start.1 = (f16[3,8,24,128]{3,2,1,0:T(8,128)(2,1)S(1)}, f16[3,8,24,128]{3,2,1,0:T(8,128)(2,1)S(1)}, u32[]{:S(2)}, u32[]{:S(2)}) collective-permute-start(f16[3,8,24,128]{3,2,1,0:T(8,128)(2,1)S(1)} %multiply_convert_fusion.1), channel_id=1, source_target_pairs={{0,1},{1,2},{2,3},{3,0},{4,5},{5,6},{6,7},{7,4},{8,9},{9,10},{10,1... | collective-permute-start | bytes 442376 | tf_op jit(solution)/shard_map/ppermute | solution.py:203
  11.8 4.9 %collective-permute-start = (f16[3,8,24,128]{3,2,1,0:T(8,128)(2,1)S(1)}, f16[3,8,24,128]{3,2,1,0:T(8,128)(2,1)S(1)}, u32[]{:S(2)}, u32[]{:S(2)}) collective-permute-start(f16[3,8,24,128]{3,2,1,0:T(8,128)(2,1)S(1)} %multiply_convert_fusion.2), channel_id=1, source_target_pairs={{0,3},{1,0},{2,1},{3,2},{4,7},{5,4},{6,5},{7,6},{8,11},{9,8},{10,9... | collective-permute-start | bytes 442376 | tf_op jit(solution)/shard_map/ppermute | solution.py:203
  16.8 7.5 %collective-permute-start.3 = (f16[2,8,24,128]{3,2,1,0:T(8,128)(2,1)S(1)}, f16[2,8,24,128]{3,2,1,0:T(8,128)(2,1)S(1)}, u32[]{:S(2)}, u32[]{:S(2)}) collective-permute-start(f16[2,8,24,128]{3,2,1,0:T(8,128)(2,1)S(1)} %get-tuple-element.13), channel_id=1, source_target_pairs={{0,28},{4,0},{8,4},{12,8},{16,12},{20,16},{24,20},{28,24},{1,29},{... | collective-permute-start | bytes 294920 | tf_op jit(solution)/shard_map/ppermute | solution.py:203
  21.1 5.5 %collective-permute-start.4 = (f16[8,24,128]{2,1,0:T(8,128)(2,1)S(1)}, f16[8,24,128]{2,1,0:T(8,128)(2,1)S(1)}, u32[]{:S(2)}, u32[]{:S(2)}) collective-permute-start(f16[8,24,128]{2,1,0:T(8,128)(2,1)S(1)} %get-tuple-element.14), channel_id=1, source_target_pairs={{0,8},{4,12},{8,16},{12,20},{16,24},{20,28},{24,0},{28,4},{1,9},{5... | collective-permute-start | bytes 147464 | tf_op jit(solution)/shard_map/ppermute | solution.py:203
  21.1 5.4 %collective-permute-start.5 = (f16[8,24,128]{2,1,0:T(8,128)(2,1)S(1)}, f16[8,24,128]{2,1,0:T(8,128)(2,1)S(1)}, u32[]{:S(2)}, u32[]{:S(2)}) collective-permute-start(f16[8,24,128]{2,1,0:T(8,128)(2,1)S(1)} %get-tuple-element.15), channel_id=1, source_target_pairs={{0,24},{4,28},{8,0},{12,4},{16,8},{20,12},{24,16},{28,20},{1,25},{... | collective-permute-start | bytes 147464 | tf_op jit(solution)/shard_map/ppermute | solution.py:203
  24.4 6.8 %collective-permute-start.2 = (f16[2,8,24,128]{3,2,1,0:T(8,128)(2,1)S(1)}, f16[2,8,24,128]{3,2,1,0:T(8,128)(2,1)S(1)}, u32[]{:S(2)}, u32[]{:S(2)}) collective-permute-start(f16[2,8,24,128]{3,2,1,0:T(8,128)(2,1)S(1)} %get-tuple-element.12), channel_id=1, source_target_pairs={{0,4},{4,8},{8,12},{12,16},{16,20},{20,24},{24,28},{28,0},{1,5},{5... | collective-permute-start | bytes 294920 | tf_op jit(solution)/shard_map/ppermute | solution.py:203
  31.4 6.4 %collective-permute-start.9 = (bf16[3,8,24,128]{3,2,1,0:T(8,128)(2,1)S(1)}, bf16[3,8,24,128]{3,2,1,0:T(8,128)(2,1)S(1)}, u32[]{:S(2)}, u32[]{:S(2)}) collective-permute-start(bf16[3,8,24,128]{3,2,1,0:T(8,128)(2,1)S(1)} %get-tuple-element.10), channel_id=1, source_target_pairs={{0,3},{1,0},{2,1},{3,2},{4,7},{5,4},{6,5},{7,6},{8,11},{9,8},{10,9... | collective-permute-start | bytes 442376 | tf_op jit(solution)/shard_map/ppermute | solution.py:203
  32.5 5.2 %collective-permute-start.8 = (bf16[3,8,24,128]{3,2,1,0:T(8,128)(2,1)S(1)}, bf16[3,8,24,128]{3,2,1,0:T(8,128)(2,1)S(1)}, u32[]{:S(2)}, u32[]{:S(2)}) collective-permute-start(bf16[3,8,24,128]{3,2,1,0:T(8,128)(2,1)S(1)} %get-tuple-element.10), channel_id=1, source_target_pairs={{0,1},{1,2},{2,3},{3,0},{4,5},{5,6},{6,7},{7,4},{8,9},{9,10},{10,1... | collective-permute-start | bytes 442376 | tf_op jit(solution)/shard_map/ppermute | solution.py:203

commit v3 on v2

v3 whole, which is shorter than its diff:
```python
import functools

import jax
import jax.numpy as jnp
from jax import lax
from jax.experimental import pallas as pl
from jax.experimental.pallas import tpu as pltpu
from jax.sharding import PartitionSpec as P


CHUNKS = 4
GROUP = 4
F32 = jnp.float32
F16 = jnp.float16
FIRST_SCALE = 8.0
SECOND_SCALE = 2.0


def partner_step(axis):
    return 1 - 2 * (lax.axis_index(axis) % 2)


def near_places(device, n_atmos, n_ocean):
    row, col = lax.axis_index("atm"), lax.axis_index("ocn")
    row_side, col_side = partner_step("atm"), partner_step("ocn")
    place = jnp.zeros_like(device)
    for i, row_step in enumerate((-row_side, 0, row_side)):
        for j, col_step in enumerate((-col_side, 0, col_side)):
            name = (row + row_step + n_atmos) % n_atmos * n_ocean + (col + col_step + n_ocean) % n_ocean
            place = jnp.where(device == name, 3 * i + j, place)
    return place


def stacked(first, second):
    spare = jnp.zeros((-first.shape[0] % 16, first.shape[1]), first.dtype)
    first = jnp.concatenate([first, spare], axis=0)
    second = jnp.concatenate([second, spare], axis=0)
    empty = jnp.zeros_like(first)
    return jnp.concatenate(
        [jnp.concatenate([first, empty], axis=1), jnp.concatenate([empty, second], axis=1)], axis=0
    )


def add_group(total, rows, targets, products):
    places = [pl.ds(pl.multiple_of(target, 8), rows) for target in targets]
    sums = []
    for k, target in enumerate(targets):
        value = products[k]
        for j in range(k):
            value = value + jnp.where(targets[j] == target, products[j], 0.0)
        sums.append(total[places[k], :] + value)
    for place, value in zip(places, sums):
        total[place, :] = value


def block_sums(blocks, source_of, target_of, load, total, rows, begin, end):
    cells = total.shape[1]
    pairs = blocks.reshape(blocks.shape[0] // 2, 2 * cells, cells)
    for group in range(begin, end, GROUP):
        products = []
        for at in range(group, group + GROUP, 2):
            sources = stacked(load(source_of(at)), load(source_of(at + 1)))
            product = jnp.dot(sources, pairs[at // 2], preferred_element_type=F32)
            half = product.shape[0] // 2
            products += [product[:rows], product[half : half + rows]]
        add_group(total, rows, [target_of(at) for at in range(group, group + GROUP)], products)


def start_all(*copies):
    for copy in copies:
        copy.start()
    return copies


def fwd_kernel(
    n_atmos, n_ocean, fields_hbm, blocks_hbm, src_hbm, dev_hbm, tile_hbm, state_hbm, mask_hbm,
    back_dev_hbm, back_src_hbm, back_dst_hbm,
    own, outer_col, inner_col, surface, back_index, same_side,
    blocks, fields, total, mask, dev_v, tile_v, place_v, back_v, src, place, sems, index_sems,
):
    tiles = own.shape[1]
    rows = fields.shape[1]
    index = start_all(
        pltpu.make_async_copy(dev_hbm, dev_v, index_sems.at[0]),
        pltpu.make_async_copy(tile_hbm, tile_v, index_sems.at[1]),
        pltpu.make_async_copy(src_hbm, src, index_sems.at[2]),
    )
    source = start_all(pltpu.make_async_copy(fields_hbm, fields, index_sems.at[3]))
    count = blocks.shape[0] // CHUNKS
    weights = start_all(*[
        pltpu.make_async_copy(
            blocks_hbm.at[pl.ds(c * count, count)], blocks.at[pl.ds(c * count, count)], sems.at[c]
        )
        for c in range(CHUNKS)
    ])
    late = start_all(
        pltpu.make_async_copy(state_hbm, surface.at[:, pl.ds(0, rows), :], index_sems.at[4]),
        pltpu.make_async_copy(mask_hbm, mask, index_sems.at[5]),
        pltpu.make_async_copy(back_dev_hbm, back_v.at[0], index_sems.at[6]),
        pltpu.make_async_copy(back_src_hbm, back_v.at[1], index_sems.at[7]),
        pltpu.make_async_copy(back_dst_hbm, back_v.at[2], index_sems.at[8]),
    )
    total[...] = jnp.zeros_like(total)
    for copy in index[:2]:
        copy.wait()
    place_v[...] = (near_places(dev_v[...], n_atmos, n_ocean) * tiles + tile_v[...]) * rows
    to_scalars = start_all(pltpu.make_async_copy(place_v, place, index_sems.at[0]))
    for copy in to_scalars + index[2:] + source:
        copy.wait()
    for c in range(CHUNKS):
        weights[c].wait()
        block_sums(
            blocks, lambda b: src[0, b], lambda b: place[0, b], lambda s: fields[s],
            total, rows, c * count, (c + 1) * count,
        )
    for row in range(3):
        for col, out in enumerate((outer_col, own, inner_col)):
            first = (row * 3 + col) * tiles * rows
            out[row] = total[first : first + tiles * rows, :].reshape(out.shape[1:])
    for copy in late:
        copy.wait()
    wet = mask[...].astype(F32)
    surface[:, rows:, :] = jnp.broadcast_to(wet[:, None, :], (tiles, surface.shape[1] - rows, wet.shape[1]))
    back_index[0] = near_places(back_v[0], n_atmos, n_ocean) * tiles + back_v[1]
    back_index[1] = back_v[2] * rows
    row = lax.axis_index("atm")
    same_side[...] = jnp.full_like(same_side, jnp.where(row % 2 == row // 2 % 2, 1, 0))


def bwd_kernel(near, blocks, index_in, out, total, index, sems):
    rows = near.shape[1]
    copies = start_all(pltpu.make_async_copy(index_in, index, sems.at[0]))
    total[...] = jnp.zeros_like(total)
    for copy in copies:
        copy.wait()
    block_sums(
        blocks, lambda b: index[0, 0, b], lambda b: index[1, 0, b], lambda s: near[s],
        total, rows, 0, blocks.shape[0],
    )
    result = pltpu.make_async_copy(total, out, sems.at[0])
    result.start()
    result.wait()


def in_hbm(*arrays):
    return [pltpu.with_memory_space_constraint(a, pltpu.HBM) for a in arrays]


def hbm():
    return pl.BlockSpec(memory_space=pl.ANY)


def vmem():
    return pl.BlockSpec(memory_space=pltpu.VMEM)


def forward(n_atmos, n_ocean, atm_fields, fwd_blocks, index, state, mask, back_index):
    fields, cells = atm_fields.shape[1:]
    count = fwd_blocks.shape[0]
    tiles = state.shape[0]
    part = (3, tiles, fields, cells)
    numbers = pltpu.VMEM((1, count), jnp.int32)
    scalars = pltpu.SMEM((1, count), jnp.int32)
    return pl.pallas_call(
        functools.partial(fwd_kernel, n_atmos, n_ocean),
        out_shape=[
            jax.ShapeDtypeStruct(part, F32),
            jax.ShapeDtypeStruct(part, F32),
            jax.ShapeDtypeStruct(part, F32),
            jax.ShapeDtypeStruct((tiles, fields + 8, cells), F32),
            jax.ShapeDtypeStruct((2, 1, count), jnp.int32),
            jax.ShapeDtypeStruct((1, 1, cells), jnp.int32),
        ],
        in_specs=[hbm()] * 10,
        out_specs=[vmem()] * 6,
        scratch_shapes=[
            pltpu.VMEM(fwd_blocks.shape, fwd_blocks.dtype),
            pltpu.VMEM(atm_fields.shape, atm_fields.dtype),
            pltpu.VMEM((9 * tiles * fields, cells), F32),
            pltpu.VMEM(mask.shape, mask.dtype),
            numbers, numbers, numbers,
            pltpu.VMEM((3, 1, count), jnp.int32),
            scalars, scalars,
            pltpu.SemaphoreType.DMA((CHUNKS,)),
            pltpu.SemaphoreType.DMA((9,)),
        ],
        compiler_params=pltpu.CompilerParams(vmem_limit_bytes=10 * 2**20),
        name="forward_blocks",
    )(*in_hbm(atm_fields, fwd_blocks, *index, state, mask, *back_index))


def backward(near, back_blocks, index, atmos_count):
    fields, cells = near.shape[1:]
    return pl.pallas_call(
        bwd_kernel,
        out_shape=jax.ShapeDtypeStruct((atmos_count * fields, cells), F32),
        in_specs=[vmem()] * 3,
        out_specs=hbm(),
        scratch_shapes=[
            pltpu.VMEM((atmos_count * fields, cells), F32),
            pltpu.SMEM(index.shape, jnp.int32),
            pltpu.SemaphoreType.DMA((1,)),
        ],
        compiler_params=pltpu.CompilerParams(vmem_limit_bytes=4 * 2**20),
        name="backward_blocks",
    )(near, back_blocks, index).reshape(atmos_count, fields, cells)


def ring_pairs(count, stride, inner):
    pairs = []
    for i in range(count):
        step = stride if (i // stride % 2 == 0) == inner else -stride
        pairs.append((i, (i + step) % count))
    return pairs


def swap(block, axis, stride, inner):
    return lax.ppermute(block, axis, ring_pairs(lax.axis_size(axis), stride, inner))


def shards(
    atm_fields, fwd_blocks, fwd_src_tile, fwd_dst_dev, fwd_dst_tile, ocean_state, wet_mask,
    back_blocks, back_src_dev, back_src_tile, back_dst_tile,
):
    n_atmos = lax.axis_size("atm")
    n_ocean = lax.axis_size("ocn")
    fields, cells = atm_fields.shape[1:]
    ocean_count = ocean_state.shape[0]
    atmos_count = atm_fields.shape[0]
    flat = (1, fwd_src_tile.shape[0])
    own, outer_col, inner_col, surface, index, same_side = forward(
        n_atmos, n_ocean, atm_fields, fwd_blocks,
        [a.reshape(flat) for a in (fwd_src_tile, fwd_dst_dev, fwd_dst_tile)],
        ocean_state, wet_mask,
        [a.reshape(flat) for a in (back_src_dev, back_src_tile, back_dst_tile)],
    )
    from_inner = swap((inner_col * FIRST_SCALE).astype(F16), "ocn", 1, True)
    from_outer = swap((outer_col * FIRST_SCALE).astype(F16), "ocn", 1, False)
    row_sums = own + (from_inner.astype(F32) + from_outer.astype(F32)) * (1.0 / FIRST_SCALE)
    sent = (row_sums * SECOND_SCALE).astype(F16)
    same = same_side > 0
    to_inner = jnp.where(same, sent[2], sent[0])
    to_outer = jnp.where(same, sent[0], sent[2])
    inner_state = swap(surface, "atm", 1, True)
    outer_state = swap(surface, "atm", 1, False)
    inner = swap(sent[1:], "atm", 1, True)
    outer = swap(sent[:2], "atm", 1, False)
    far_inner = swap(to_inner, "atm", 2, True)
    far_outer = swap(to_outer, "atm", 2, False)
    direct = jnp.stack([outer[1], inner[1], inner[0]]).astype(F32)
    other = jnp.stack([jnp.where(same, far_outer, far_inner), outer[0], jnp.where(same, far_inner, far_outer)]).astype(F32)
    sums = row_sums + (direct + other) * (1.0 / SECOND_SCALE)
    surface = jnp.stack([outer_state, surface, inner_state])
    wet = surface[:, :, fields : fields + 1]
    response = (wet * jnp.tanh(surface[:, :, :fields] + sums)).astype(jnp.bfloat16)
    inner_near = swap(response, "ocn", 1, True)
    outer_near = swap(response, "ocn", 1, False)
    near = jnp.stack([outer_near, response, inner_near], axis=1).reshape(9 * ocean_count, fields, cells)
    return (sums[1], backward(near, back_blocks, index, atmos_count))


def solution(mesh):
    part = ("atm", "ocn")
    three, two, one = P(part, None, None), P(part, None), P(part)
    in_specs = (three, three, one, two, one, three, two, three, two, one, one)
    return jax.shard_map(shards, mesh=mesh, in_specs=in_specs, out_specs=(three, three), check_vma=False)
```

time: 42.3 us -> 36.6 us (0.87); the launches traced: 41.5 us -> 36.4 us
  waiting for transfers between devices: 15.3 us -> 12.1 us
  starting transfers between devices: 16.9 us -> 15.6 us
  Pallas kernels: 7.38 us -> 6.67 us
    ppermute x10, waiting for transfers between devices: 15.3 us -> 12.1 us  [swap(): lax.ppermute(block, axis, ring_pairs(lax.axis_size(axis), stride, inner))]
    ppermute x10, starting transfers between devices: 16.9 us -> 15.6 us  [swap(): lax.ppermute(block, axis, ring_pairs(lax.axis_size(axis), stride, inner))]
    pallas_call x1, Pallas kernels: 3.6 us -> 2.79 us  [backward(): pl.pallas_call(bwd_kernel, out_shape=jax.ShapeDtypeStruct((atmos_count *...]
where the time goes in v3:
time: 36.6 us; the launch traced here: 36.4 us
  starting transfers between devices  15.6 us (43%)
  waiting for transfers between devices  12.1 us (33%)
  Pallas kernels  6.67 us (18%)
  local copies, waits for them, and re-layouts  0.78 us (2%)
  between operations  0.78 us (2%)
  other arithmetic  0.49 us (1%)
    ppermute x10, starting transfers between devices, swap(): lax.ppermute(block, axis, ring_pairs(lax.axis_size(axis), stride, inner))  15.6 us
    ppermute x10, waiting for transfers between devices, swap(): lax.ppermute(block, axis, ring_pairs(lax.axis_size(axis), stride, inner))  12.1 us
    pallas_call x1, Pallas kernels, forward(): pl.pallas_call(functools.partial(fwd_kernel, n_atmos, n_ocean), out_shape...  3.88 us
    pallas_call x1, Pallas kernels, backward(): pl.pallas_call(bwd_kernel, out_shape=jax.ShapeDtypeStruct((atmos_count *...  2.79 us
  transfers between devices with their start and end apart: 10, of which 5 were waited for; matrix products, arithmetic and copies ran while one was open for 2% of the time, Pallas kernels for 0%

profile of v3, /device:TPU:1, one launch (start us, length us, event | category | flops | bytes accessed | tf_op | source)
XLA Modules:
  0.0 36.4 jit_solution(17650626707852566886)
XLA Ops:
  0.6 0.0 slice-start.1
  0.7 3.9 %forward_blocks.1 = (f32[3,8,24,128]{3,2,1,0:T(8,128)S(1)}, f32[3,8,24,128]{3,2,1,0:T(8,128)S(1)}, f32[3,8,24,128]{3,2,1,0:T(8,128)S(1)}, f32[8,32,128]{2,1,0:T(...) custom-call(bf16[128,24,128]{2,1,0:T(8,128)(2,1)} %fields_hbm.1, bf16[192,128,128]{2,1,0:T(8,128)(2,1)} %blocks_hbm.1, ...), custom_call_target="tpu_custom_call" | custom-call | tf_op jit(solution)/shard_map/forward_blocks/pallas_call | solution.py:164
  4.5 2.1 %collective-permute-start.7 = (f32[8,32,128]{2,1,0:T(8,128)S(1)}, f32[8,32,128]{2,1,0:T(8,128)S(1)}, u32[]{:S(2)}, u32[]{:S(2)}) collective-permute-start(f32[8,32,128]{2,1,0:T(8,128)S(1)} %get-tuple-element.12), channel_id=1, source_target_pairs={{0,4},{4,0},{8,12},{12,8},{16,20},{20,16},{24,28},{28,24},{1,5},{5... | collective-permute-start | bytes 393224 | tf_op jit(solution)/shard_map/ppermute | solution.py:218
  6.7 3.3 %collective-permute-start.6 = (f32[8,32,128]{2,1,0:T(8,128)S(1)}, f32[8,32,128]{2,1,0:T(8,128)S(1)}, u32[]{:S(2)}, u32[]{:S(2)}) collective-permute-start(f32[8,32,128]{2,1,0:T(8,128)S(1)} %get-tuple-element.12), channel_id=1, source_target_pairs={{0,28},{4,8},{8,4},{12,16},{16,12},{20,24},{24,20},{28,0},{1,29},{... | collective-permute-start | bytes 393224 | tf_op jit(solution)/shard_map/ppermute | solution.py:218
  10.0 2.4 %collective-permute-start.1 = (f16[3,8,24,128]{3,2,1,0:T(8,128)(2,1)S(1)}, f16[3,8,24,128]{3,2,1,0:T(8,128)(2,1)S(1)}, u32[]{:S(2)}, u32[]{:S(2)}) collective-permute-start(f16[3,8,24,128]{3,2,1,0:T(8,128)(2,1)S(1)} %multiply_convert_fusion.1), channel_id=1, source_target_pairs={{0,3},{1,2},{2,1},{3,0},{4,7},{5,6},{6,5},{7,4},{8,11},{9,10},{10,... | collective-permute-start | bytes 442376 | tf_op jit(solution)/shard_map/ppermute | solution.py:218
  12.4 0.1 collective-permute-start
  12.5 0.0 collective-permute-done.7
  12.5 0.7 %collective-permute-done.6 = f32[8,32,128]{2,1,0:T(8,128)S(1)} collective-permute-done((f32[8,32,128]{2,1,0:T(8,128)S(1)}, f32[8,32,128]{2,1,0:T(8,128)S(1)}, u32[]{:S(2)}, u32[]{:S(2)}) %collective-permute-start.6) | collective-permute-done | bytes 131104 | tf_op jit(solution)/shard_map/ppermute | solution.py:218
  13.2 3.8 %collective-permute-done.1 = f16[3,8,24,128]{3,2,1,0:T(8,128)(2,1)S(1)} collective-permute-done((f16[3,8,24,128]{3,2,1,0:T(8,128)(2,1)S(1)}, f16[3,8,24,128]{3,2,1,0:T(8,128)(2,1)S(1)}, u32[]{:S(2)}, u32[]{:S(2)}) %collective-permute-start.1) | collective-permute-done | bytes 147488 | tf_op jit(solution)/shard_map/ppermute | solution.py:218
  17.0 0.0 collective-permute-done
  17.0 0.1 multiply_convert_fusion
  17.1 0.2 collective-permute-start.4
  17.4 1.7 %collective-permute-start.3 = (f16[2,8,24,128]{3,2,1,0:T(8,128)(2,1)S(1)}, f16[2,8,24,128]{3,2,1,0:T(8,128)(2,1)S(1)}, u32[]{:S(2)}, u32[]{:S(2)}) collective-permute-start(f16[2,8,24,128]{3,2,1,0:T(8,128)(2,1)S(1)} %get-tuple-element.18), channel_id=1, source_target_pairs={{0,4},{4,0},{8,12},{12,8},{16,20},{20,16},{24,28},{28,24},{1,5},{5... | collective-permute-start | bytes 294920 | tf_op jit(solution)/shard_map/ppermute | solution.py:218
  19.1 2.7 %collective-permute-start.2 = (f16[2,8,24,128]{3,2,1,0:T(8,128)(2,1)S(1)}, f16[2,8,24,128]{3,2,1,0:T(8,128)(2,1)S(1)}, u32[]{:S(2)}, u32[]{:S(2)}) collective-permute-start(f16[2,8,24,128]{3,2,1,0:T(8,128)(2,1)S(1)} %get-tuple-element.19), channel_id=1, source_target_pairs={{0,28},{4,8},{8,4},{12,16},{16,12},{20,24},{24,20},{28,0},{1,29},{... | collective-permute-start | bytes 294920 | tf_op jit(solution)/shard_map/ppermute | solution.py:218
  21.7 0.3 collective-permute-done.4
  22.1 0.0 collective-permute-done.3
  22.1 3.1 %collective-permute-done.2 = f16[2,8,24,128]{3,2,1,0:T(8,128)(2,1)S(1)} collective-permute-done((f16[2,8,24,128]{3,2,1,0:T(8,128)(2,1)S(1)}, f16[2,8,24,128]{3,2,1,0:T(8,128)(2,1)S(1)}, u32[]{:S(2)}, u32[]{:S(2)}) %collective-permute-start.2) | collective-permute-done | bytes 98336 | tf_op jit(solution)/shard_map/ppermute | solution.py:218
  25.3 0.2 fusion.3
  25.5 2.4 %collective-permute-start.9 = (bf16[3,8,24,128]{3,2,1,0:T(8,128)(2,1)S(1)}, bf16[3,8,24,128]{3,2,1,0:T(8,128)(2,1)S(1)}, u32[]{:S(2)}, u32[]{:S(2)}) collective-permute-start(bf16[3,8,24,128]{3,2,1,0:T(8,128)(2,1)S(1)} %get-tuple-element.14), channel_id=1, source_target_pairs={{0,1},{1,0},{2,3},{3,2},{4,5},{5,4},{6,7},{7,6},{8,9},{9,8},{10,11... | collective-permute-start | bytes 442376 | tf_op jit(solution)/shard_map/ppermute | solution.py:218
  27.9 0.7 %collective-permute-start.8 = (bf16[3,8,24,128]{3,2,1,0:T(8,128)(2,1)S(1)}, bf16[3,8,24,128]{3,2,1,0:T(8,128)(2,1)S(1)}, u32[]{:S(2)}, u32[]{:S(2)}) collective-permute-start(bf16[3,8,24,128]{3,2,1,0:T(8,128)(2,1)S(1)} %get-tuple-element.14), channel_id=1, source_target_pairs={{0,3},{1,2},{2,1},{3,0},{4,7},{5,6},{6,5},{7,4},{8,11},{9,10},{10,... | collective-permute-start | bytes 442376 | tf_op jit(solution)/shard_map/ppermute | solution.py:218
  28.6 0.6 %slice_bitcast_fusion = f32[8,24,128]{2,1,0:T(8,128)} fusion(f32[3,8,24,128]{3,2,1,0:T(8,128)S(1)} %get-tuple-element.15), kind=kLoop, calls=%fused_computation.12 | loop fusion | bytes 196608 | tf_op jit(solution)/shard_map/squeeze | solution.py:259
  29.3 4.2 %collective-permute-done.8 = bf16[3,8,24,128]{3,2,1,0:T(8,128)(2,1)S(1)} collective-permute-done((bf16[3,8,24,128]{3,2,1,0:T(8,128)(2,1)S(1)}, bf16[3,8,24,128]{3,2,1,0:T(8,128)(2,1)S(1)}, u32[]{:S(2)}, u32[]{:S(2)}) %collective-permute-start.8) | collective-permute-done | bytes 147488 | tf_op jit(solution)/shard_map/ppermute | solution.py:218
  33.5 0.1 pad_maximum_fusion
  33.6 2.8 %backward_blocks.1 = f32[3072,128]{1,0:T(8,128)} custom-call(bf16[72,24,128]{2,1,0:T(8,128)(2,1)S(1)} %bitcast.37, bf16[192,128,128]{2,1,0:T(8,128)(2,1)S(1)} %bitcast.36, s32[2,1,192]{2,1,0:T(1,128)S(1)} %get-tuple-element.13.index_in), custom_call_target="tpu_custom_call" | custom-call | tf_op jit(solution)/shard_map/backward_blocks/pallas_call | solution.py:194
  (17 shorter events, 0.3 us)
Async XLA Ops:
  0.6 32.9 %slice-start = ((s8[6291456]{0:T(1024)(128)(4,1)}), s8[4194304]{0:T(1024)(128)(4,1)S(1)}, s32[]{:S(2)}) async-start(s8[6291456]{0:T(1024)(128)(4,1)} %bitcast.35), calls=%async_computation | async-start | bytes 8388608
  0.6 32.9 %slice-start.1 = ((s8[6291456]{0:T(1024)(128)(4,1)}), s8[2097152]{0:T(1024)(128)(4,1)S(1)}, s32[]{:S(2)}) async-start(s8[6291456]{0:T(1024)(128)(4,1)} %bitcast.35), calls=%async_computation.1 | async-start | bytes 4194304
  4.5 8.0 %collective-permute-start.7 = (f32[8,32,128]{2,1,0:T(8,128)S(1)}, f32[8,32,128]{2,1,0:T(8,128)S(1)}, u32[]{:S(2)}, u32[]{:S(2)}) collective-permute-start(f32[8,32,128]{2,1,0:T(8,128)S(1)} %get-tuple-element.12), channel_id=1, source_target_pairs={{0,4},{4,0},{8,12},{12,8},{16,20},{20,16},{24,28},{28,24},{1,5},{5... | collective-permute-start | bytes 393224 | tf_op jit(solution)/shard_map/ppermute | solution.py:218
  6.7 6.5 %collective-permute-start.6 = (f32[8,32,128]{2,1,0:T(8,128)S(1)}, f32[8,32,128]{2,1,0:T(8,128)S(1)}, u32[]{:S(2)}, u32[]{:S(2)}) collective-permute-start(f32[8,32,128]{2,1,0:T(8,128)S(1)} %get-tuple-element.12), channel_id=1, source_target_pairs={{0,28},{4,8},{8,4},{12,16},{16,12},{20,24},{24,20},{28,0},{1,29},{... | collective-permute-start | bytes 393224 | tf_op jit(solution)/shard_map/ppermute | solution.py:218
  10.0 7.0 %collective-permute-start.1 = (f16[3,8,24,128]{3,2,1,0:T(8,128)(2,1)S(1)}, f16[3,8,24,128]{3,2,1,0:T(8,128)(2,1)S(1)}, u32[]{:S(2)}, u32[]{:S(2)}) collective-permute-start(f16[3,8,24,128]{3,2,1,0:T(8,128)(2,1)S(1)} %multiply_convert_fusion.1), channel_id=1, source_target_pairs={{0,3},{1,2},{2,1},{3,0},{4,7},{5,6},{6,5},{7,4},{8,11},{9,10},{10,... | collective-permute-start | bytes 442376 | tf_op jit(solution)/shard_map/ppermute | solution.py:218
  12.4 4.6 %collective-permute-start = (f16[3,8,24,128]{3,2,1,0:T(8,128)(2,1)S(1)}, f16[3,8,24,128]{3,2,1,0:T(8,128)(2,1)S(1)}, u32[]{:S(2)}, u32[]{:S(2)}) collective-permute-start(f16[3,8,24,128]{3,2,1,0:T(8,128)(2,1)S(1)} %multiply_convert_fusion.2), channel_id=1, source_target_pairs={{0,1},{1,0},{2,3},{3,2},{4,5},{5,4},{6,7},{7,6},{8,9},{9,8},{10,11... | collective-permute-start | bytes 442376 | tf_op jit(solution)/shard_map/ppermute | solution.py:218
  17.1 4.9 %collective-permute-start.4 = (f16[8,24,128]{2,1,0:T(8,128)(2,1)S(1)}, f16[8,24,128]{2,1,0:T(8,128)(2,1)S(1)}, u32[]{:S(2)}, u32[]{:S(2)}) collective-permute-start(f16[8,24,128]{2,1,0:T(8,128)(2,1)S(1)} %get-tuple-element.16), channel_id=1, source_target_pairs={{0,24},{4,28},{8,16},{12,20},{16,8},{20,12},{24,0},{28,4},{1,25},{... | collective-permute-start | bytes 147464 | tf_op jit(solution)/shard_map/ppermute | solution.py:218
  17.3 4.7 %collective-permute-start.5 = (f16[8,24,128]{2,1,0:T(8,128)(2,1)S(1)}, f16[8,24,128]{2,1,0:T(8,128)(2,1)S(1)}, u32[]{:S(2)}, u32[]{:S(2)}) collective-permute-start(f16[8,24,128]{2,1,0:T(8,128)(2,1)S(1)} %get-tuple-element.17), channel_id=1, source_target_pairs={{0,8},{4,12},{8,0},{12,4},{16,24},{20,28},{24,16},{28,20},{1,9},{5... | collective-permute-start | bytes 147464 | tf_op jit(solution)/shard_map/ppermute | solution.py:218
  17.4 4.7 %collective-permute-start.3 = (f16[2,8,24,128]{3,2,1,0:T(8,128)(2,1)S(1)}, f16[2,8,24,128]{3,2,1,0:T(8,128)(2,1)S(1)}, u32[]{:S(2)}, u32[]{:S(2)}) collective-permute-start(f16[2,8,24,128]{3,2,1,0:T(8,128)(2,1)S(1)} %get-tuple-element.18), channel_id=1, source_target_pairs={{0,4},{4,0},{8,12},{12,8},{16,20},{20,16},{24,28},{28,24},{1,5},{5... | collective-permute-start | bytes 294920 | tf_op jit(solution)/shard_map/ppermute | solution.py:218
  19.1 6.2 %collective-permute-start.2 = (f16[2,8,24,128]{3,2,1,0:T(8,128)(2,1)S(1)}, f16[2,8,24,128]{3,2,1,0:T(8,128)(2,1)S(1)}, u32[]{:S(2)}, u32[]{:S(2)}) collective-permute-start(f16[2,8,24,128]{3,2,1,0:T(8,128)(2,1)S(1)} %get-tuple-element.19), channel_id=1, source_target_pairs={{0,28},{4,8},{8,4},{12,16},{16,12},{20,24},{24,20},{28,0},{1,29},{... | collective-permute-start | bytes 294920 | tf_op jit(solution)/shard_map/ppermute | solution.py:218
  25.5 3.8 %collective-permute-start.9 = (bf16[3,8,24,128]{3,2,1,0:T(8,128)(2,1)S(1)}, bf16[3,8,24,128]{3,2,1,0:T(8,128)(2,1)S(1)}, u32[]{:S(2)}, u32[]{:S(2)}) collective-permute-start(bf16[3,8,24,128]{3,2,1,0:T(8,128)(2,1)S(1)} %get-tuple-element.14), channel_id=1, source_target_pairs={{0,1},{1,0},{2,3},{3,2},{4,5},{5,4},{6,7},{7,6},{8,9},{9,8},{10,11... | collective-permute-start | bytes 442376 | tf_op jit(solution)/shard_map/ppermute | solution.py:218
  27.9 5.5 %collective-permute-start.8 = (bf16[3,8,24,128]{3,2,1,0:T(8,128)(2,1)S(1)}, bf16[3,8,24,128]{3,2,1,0:T(8,128)(2,1)S(1)}, u32[]{:S(2)}, u32[]{:S(2)}) collective-permute-start(bf16[3,8,24,128]{3,2,1,0:T(8,128)(2,1)S(1)} %get-tuple-element.14), channel_id=1, source_target_pairs={{0,3},{1,2},{2,1},{3,0},{4,7},{5,6},{6,5},{7,4},{8,11},{9,10},{10,... | collective-permute-start | bytes 442376 | tf_op jit(solution)/shard_map/ppermute | solution.py:218

commit v4 on v3

--- a/solution.py
+++ b/solution.py
@@ -27,7 +27,7 @@
     for i, row_step in enumerate((-row_side, 0, row_side)):
         for j, col_step in enumerate((-col_side, 0, col_side)):
             name = (row + row_step + n_atmos) % n_atmos * n_ocean + (col + col_step + n_ocean) % n_ocean
-            place = jnp.where(device == name, 3 * i + j, place)
+            place = jnp.where(device == name, 3 * j + i, place)
     return place
 
 
@@ -53,17 +53,17 @@
         total[place, :] = value
 
 
-def block_sums(blocks, source_of, target_of, load, total, rows, begin, end):
-    cells = total.shape[1]
-    pairs = blocks.reshape(blocks.shape[0] // 2, 2 * cells, cells)
-    for group in range(begin, end, GROUP):
+def block_sums(begin, end, block_of, weights, load, source_of, target_of, total, rows):
+    for group in range(0, end, GROUP):
+        numbers = [block_of(begin + at) for at in range(group, group + GROUP)]
         products = []
-        for at in range(group, group + GROUP, 2):
-            sources = stacked(load(source_of(at)), load(source_of(at + 1)))
-            product = jnp.dot(sources, pairs[at // 2], preferred_element_type=F32)
+        for first, second in zip(numbers[::2], numbers[1::2]):
+            sources = stacked(load(source_of(first)), load(source_of(second)))
+            pair = weights(first, second)
+            product = jnp.dot(sources, pair, preferred_element_type=F32)
             half = product.shape[0] // 2
             products += [product[:rows], product[half : half + rows]]
-        add_group(total, rows, [target_of(at) for at in range(group, group + GROUP)], products)
+        add_group(total, rows, [target_of(number) for number in numbers], products)
 
 
 def start_all(*copies):
@@ -75,10 +75,10 @@
 def fwd_kernel(
     n_atmos, n_ocean, fields_hbm, blocks_hbm, src_hbm, dev_hbm, tile_hbm, state_hbm, mask_hbm,
     back_dev_hbm, back_src_hbm, back_dst_hbm,
-    own, outer_col, inner_col, surface, back_index, same_side,
-    blocks, fields, total, mask, dev_v, tile_v, place_v, back_v, src, place, sems, index_sems,
+    total, surface, back_index, same_side,
+    blocks, fields, mask, dev_v, tile_v, place_v, back_v, src, place, sems, index_sems,
 ):
-    tiles = own.shape[1]
+    tiles = mask.shape[0]
     rows = fields.shape[1]
     index = start_all(
         pltpu.make_async_copy(dev_hbm, dev_v, index_sems.at[0]),
@@ -94,7 +94,7 @@
         for c in range(CHUNKS)
     ])
     late = start_all(
-        pltpu.make_async_copy(state_hbm, surface.at[:, pl.ds(0, rows), :], index_sems.at[4]),
+        pltpu.make_async_copy(state_hbm, surface.at[pl.ds(0, tiles * rows), :], index_sems.at[4]),
         pltpu.make_async_copy(mask_hbm, mask, index_sems.at[5]),
         pltpu.make_async_copy(back_dev_hbm, back_v.at[0], index_sems.at[6]),
         pltpu.make_async_copy(back_src_hbm, back_v.at[1], index_sems.at[7]),
@@ -107,36 +107,72 @@
     to_scalars = start_all(pltpu.make_async_copy(place_v, place, index_sems.at[0]))
     for copy in to_scalars + index[2:] + source:
         copy.wait()
+    pairs = blocks.reshape(blocks.shape[0] // 2, 2 * blocks.shape[1], blocks.shape[2])
     for c in range(CHUNKS):
         weights[c].wait()
         block_sums(
-            blocks, lambda b: src[0, b], lambda b: place[0, b], lambda s: fields[s],
-            total, rows, c * count, (c + 1) * count,
+            c * count, count, lambda b: b, lambda b, _: pairs[b // 2], lambda s: fields[s],
+            lambda b: src[0, b], lambda b: place[0, b], total, rows,
         )
-    for row in range(3):
-        for col, out in enumerate((outer_col, own, inner_col)):
-            first = (row * 3 + col) * tiles * rows
-            out[row] = total[first : first + tiles * rows, :].reshape(out.shape[1:])
     for copy in late:
         copy.wait()
-    wet = mask[...].astype(F32)
-    surface[:, rows:, :] = jnp.broadcast_to(wet[:, None, :], (tiles, surface.shape[1] - rows, wet.shape[1]))
+    surface[tiles * rows :, :] = mask[...].astype(F32)
     back_index[0] = near_places(back_v[0], n_atmos, n_ocean) * tiles + back_v[1]
     back_index[1] = back_v[2] * rows
     row = lax.axis_index("atm")
     same_side[...] = jnp.full_like(same_side, jnp.where(row % 2 == row // 2 % 2, 1, 0))
 
 
-def bwd_kernel(near, blocks, index_in, out, total, index, sems):
+def run_step(count):
+    return next(step for step in (48, 16, 8, 4) if count % step == 0)
+
+
+def run_blocks(first, last, near, blocks, index, order, total, skipped):
     rows = near.shape[1]
-    copies = start_all(pltpu.make_async_copy(index_in, index, sems.at[0]))
+    step = run_step(blocks.shape[0])
+
+    def trip(at, carry):
+        block_sums(
+            at * step, step, lambda b: order[b],
+            lambda b, c: jnp.concatenate([blocks[b], blocks[c]], axis=0), lambda s: near[s],
+            lambda b: index[0, 0, b] - skipped, lambda b: index[1, 0, b], total, rows,
+        )
+        return carry
+
+    lax.fori_loop(first, last, trip, 0)
+
+
+def early_kernel(tiles, near, blocks, index_in, total, order_out, index, order, sems):
+    count = blocks.shape[0]
+    outer = 3 * tiles
+    copy = pltpu.make_async_copy(index_in, index, sems.at[0])
+    copy.start()
     total[...] = jnp.zeros_like(total)
+    copy.wait()
+
+    def place_block(b, ends):
+        front, back = ends
+        far = (index[0, 0, b] < outer).astype(jnp.int32)
+        order[jnp.where(far == 1, back, front)] = b
+        return front + 1 - far, back - far
+
+    ready, _ = lax.fori_loop(0, count, place_block, (jnp.int32(0), jnp.int32(count - 1)), unroll=8)
+    trips = ready // run_step(count)
+    order[count] = trips
+    copy = pltpu.make_async_copy(order, order_out, sems.at[0])
+    copy.start()
+    run_blocks(0, trips, near, blocks, index, order, total, outer)
+    copy.wait()
+
+
+def late_kernel(near, blocks, index_in, order_in, total_in, total, out, index, order, sems):
+    count = blocks.shape[0]
+    copies = start_all(
+        pltpu.make_async_copy(index_in, index, sems.at[0]), pltpu.make_async_copy(order_in, order, sems.at[1])
+    )
     for copy in copies:
         copy.wait()
-    block_sums(
-        blocks, lambda b: index[0, 0, b], lambda b: index[1, 0, b], lambda s: near[s],
-        total, rows, 0, blocks.shape[0],
-    )
+    run_blocks(order[count], count // run_step(count), near, blocks, index, order, total, 0)
     result = pltpu.make_async_copy(total, out, sems.at[0])
     result.start()
     result.wait()
@@ -158,25 +194,21 @@
     fields, cells = atm_fields.shape[1:]
     count = fwd_blocks.shape[0]
     tiles = state.shape[0]
-    part = (3, tiles, fields, cells)
     numbers = pltpu.VMEM((1, count), jnp.int32)
     scalars = pltpu.SMEM((1, count), jnp.int32)
     return pl.pallas_call(
         functools.partial(fwd_kernel, n_atmos, n_ocean),
         out_shape=[
-            jax.ShapeDtypeStruct(part, F32),
-            jax.ShapeDtypeStruct(part, F32),
-            jax.ShapeDtypeStruct(part, F32),
-            jax.ShapeDtypeStruct((tiles, fields + 8, cells), F32),
+            jax.ShapeDtypeStruct((9 * tiles * fields, cells), F32),
+            jax.ShapeDtypeStruct((tiles * fields + tiles, cells), F32),
             jax.ShapeDtypeStruct((2, 1, count), jnp.int32),
             jax.ShapeDtypeStruct((1, 1, cells), jnp.int32),
         ],
         in_specs=[hbm()] * 10,
-        out_specs=[vmem()] * 6,
+        out_specs=[vmem()] * 4,
         scratch_shapes=[
             pltpu.VMEM(fwd_blocks.shape, fwd_blocks.dtype),
             pltpu.VMEM(atm_fields.shape, atm_fields.dtype),
-            pltpu.VMEM((9 * tiles * fields, cells), F32),
             pltpu.VMEM(mask.shape, mask.dtype),
             numbers, numbers, numbers,
             pltpu.VMEM((3, 1, count), jnp.int32),
@@ -186,24 +218,49 @@
         ],
         compiler_params=pltpu.CompilerParams(vmem_limit_bytes=10 * 2**20),
         name="forward_blocks",
-    )(*in_hbm(atm_fields, fwd_blocks, *index, state, mask, *back_index))
-
-
-def backward(near, back_blocks, index, atmos_count):
+    )(*in_hbm(atm_fields, fwd_blocks, *index, state.reshape(tiles * fields, cells), mask, *back_index))
+
+
+def backward_early(near, back_blocks, index, tiles, atmos_count):
     fields, cells = near.shape[1:]
+    count = back_blocks.shape[0]
+    listed = (count + 64,)
     return pl.pallas_call(
-        bwd_kernel,
-        out_shape=jax.ShapeDtypeStruct((atmos_count * fields, cells), F32),
+        functools.partial(early_kernel, tiles),
+        out_shape=[
+            jax.ShapeDtypeStruct((atmos_count * fields, cells), F32),
+            jax.ShapeDtypeStruct(listed, jnp.int32),
+        ],
         in_specs=[vmem()] * 3,
-        out_specs=hbm(),
+        out_specs=[vmem(), vmem()],
         scratch_shapes=[
-            pltpu.VMEM((atmos_count * fields, cells), F32),
             pltpu.SMEM(index.shape, jnp.int32),
+            pltpu.SMEM(listed, jnp.int32),
             pltpu.SemaphoreType.DMA((1,)),
         ],
+        compiler_params=pltpu.CompilerParams(vmem_limit_bytes=4 * 2**20),
+        name="early_blocks",
+    )(near, back_blocks, index)
+
+
+def backward_late(near, back_blocks, index, order, total):
+    fields, cells = near.shape[1:]
+    shape = jax.ShapeDtypeStruct(total.shape, F32)
+    _, out = pl.pallas_call(
+        late_kernel,
+        out_shape=[shape, shape],
+        in_specs=[vmem()] * 5,
+        out_specs=[vmem(), hbm()],
+        scratch_shapes=[
+            pltpu.SMEM(index.shape, jnp.int32),
+            pltpu.SMEM(order.shape, jnp.int32),
+            pltpu.SemaphoreType.DMA((2,)),
+        ],
+        input_output_aliases={4: 0},
         compiler_params=pltpu.CompilerParams(vmem_limit_bytes=4 * 2**20),
         name="backward_blocks",
-    )(near, back_blocks, index).reshape(atmos_count, fields, cells)
+    )(near, back_blocks, index, order, total)
+    return out.reshape(-1, fields, cells)
 
 
 def ring_pairs(count, stride, inner):
@@ -228,12 +285,13 @@
     ocean_count = ocean_state.shape[0]
     atmos_count = atm_fields.shape[0]
     flat = (1, fwd_src_tile.shape[0])
-    own, outer_col, inner_col, surface, index, same_side = forward(
+    totals, surface, index, same_side = forward(
         n_atmos, n_ocean, atm_fields, fwd_blocks,
         [a.reshape(flat) for a in (fwd_src_tile, fwd_dst_dev, fwd_dst_tile)],
         ocean_state, wet_mask,
         [a.reshape(flat) for a in (back_src_dev, back_src_tile, back_dst_tile)],
     )
+    outer_col, own, inner_col = totals.reshape(3, 3, ocean_count, fields, cells)
     from_inner = swap((inner_col * FIRST_SCALE).astype(F16), "ocn", 1, True)
     from_outer = swap((outer_col * FIRST_SCALE).astype(F16), "ocn", 1, False)
     row_sums = own + (from_inner.astype(F32) + from_outer.astype(F32)) * (1.0 / FIRST_SCALE)
@@ -251,12 +309,15 @@
     other = jnp.stack([jnp.where(same, far_outer, far_inner), outer[0], jnp.where(same, far_inner, far_outer)]).astype(F32)
     sums = row_sums + (direct + other) * (1.0 / SECOND_SCALE)
     surface = jnp.stack([outer_state, surface, inner_state])
-    wet = surface[:, :, fields : fields + 1]
-    response = (wet * jnp.tanh(surface[:, :, :fields] + sums)).astype(jnp.bfloat16)
+    state = surface[:, : ocean_count * fields].reshape(sums.shape)
+    wet = surface[:, ocean_count * fields :].reshape(3, ocean_count, 1, cells)
+    response = (wet * jnp.tanh(state + sums)).astype(jnp.bfloat16)
     inner_near = swap(response, "ocn", 1, True)
     outer_near = swap(response, "ocn", 1, False)
-    near = jnp.stack([outer_near, response, inner_near], axis=1).reshape(9 * ocean_count, fields, cells)
-    return (sums[1], backward(near, back_blocks, index, atmos_count))
+    ready = jnp.stack([response, inner_near]).reshape(6 * ocean_count, fields, cells)
+    total, order = backward_early(ready, back_blocks, index, ocean_count, atmos_count)
+    near = jnp.stack([outer_near, response, inner_near]).reshape(9 * ocean_count, fields, cells)
+    return (sums[1], backward_late(near, back_blocks, index, order, total))
 
 
 def solution(mesh):

time: 36.6 us -> 38.4 us (1.049)
  Pallas kernels: 6.67 us -> 8.49 us
    pallas_call x1 -> x2, Pallas kernels: 2.79 us -> 4.67 us  [the longest x1 2.52 us: backward_early(): pl.pallas_call(functools.partial(early_kernel, tiles), out_shape=[jax.Sha...]
where the time goes in v4:
time: 38.4 us; the launch traced here: 38.2 us
  starting transfers between devices  15.5 us (40%)
  waiting for transfers between devices  12.2 us (32%)
  Pallas kernels  8.49 us (22%)
  between operations  0.76 us (2%)
  local copies, waits for them, and re-layouts  0.74 us (2%)
  other arithmetic  0.5 us (1%)
    ppermute x10, starting transfers between devices, swap(): lax.ppermute(block, axis, ring_pairs(lax.axis_size(axis), stride, inner))  15.5 us
    ppermute x10, waiting for transfers between devices, swap(): lax.ppermute(block, axis, ring_pairs(lax.axis_size(axis), stride, inner))  12.2 us
    pallas_call x1, Pallas kernels, forward(): pl.pallas_call(functools.partial(fwd_kernel, n_atmos, n_ocean), out_shape...  3.82 us
    pallas_call x1, Pallas kernels, backward_early(): pl.pallas_call(functools.partial(early_kernel, tiles), out_shape=[jax.Sha...  2.52 us
    pallas_call x1, Pallas kernels, backward_late(): pl.pallas_call(late_kernel, out_shape=[shape, shape], in_specs=[vmem()] *...  2.15 us
  transfers between devices with their start and end apart: 10, of which 5 were waited for; matrix products, arithmetic and copies ran while one was open for 2% of the time, Pallas kernels for 0%

profile of v4, /device:TPU:1, one launch (start us, length us, event | category | flops | bytes accessed | tf_op | source)
XLA Modules:
  0.0 38.2 jit_solution(3345209899457689970)
XLA Ops:
  0.6 0.0 slice-start
  0.6 3.8 %forward_blocks.1 = (f32[1728,128]{1,0:T(8,128)S(1)}, f32[200,128]{1,0:T(8,128)S(1)}, s32[2,1,192]{2,1,0:T(1,128)S(1)}, s32[1,1,128]{2,1,0:T(1,128)S(1)}) custom-call(bf16[128,24,128]{2,1,0:T(8,128)(2,1)} %fields_hbm.1, bf16[192,128,128]{2,1,0:T(8,128)(2,1)} %blocks_hbm.1, s32[1,192]{1,0:T(1,128)} %bitcast.61, s32[1,192]{1,0:T(1,128)} %bitcast.62, ...), custom_call_target="tpu_custom_call" | custom-call | tf_op jit(solution)/shard_map/forward_blocks/pallas_call | solution.py:199
  4.5 2.1 %collective-permute-start.7 = (f32[200,128]{1,0:T(8,128)S(1)}, f32[200,128]{1,0:T(8,128)S(1)}, u32[]{:S(2)}, u32[]{:S(2)}) collective-permute-start(f32[200,128]{1,0:T(8,128)S(1)} %get-tuple-element.11), channel_id=1, source_target_pairs={{0,4},{4,0},{8,12},{12,8},{16,20},{20,16},{24,28},{28,24},{1,5},{5... | collective-permute-start | bytes 307208 | tf_op jit(solution)/shard_map/ppermute | solution.py:275
  6.6 3.3 %collective-permute-start.6 = (f32[200,128]{1,0:T(8,128)S(1)}, f32[200,128]{1,0:T(8,128)S(1)}, u32[]{:S(2)}, u32[]{:S(2)}) collective-permute-start(f32[200,128]{1,0:T(8,128)S(1)} %get-tuple-element.11), channel_id=1, source_target_pairs={{0,28},{4,8},{8,4},{12,16},{16,12},{20,24},{24,20},{28,0},{1,29},{... | collective-permute-start | bytes 307208 | tf_op jit(solution)/shard_map/ppermute | solution.py:275
  9.9 0.1 multiply_convert_fusion.3
  9.9 2.4 %collective-permute-start.1 = (f16[3,8,24,128]{3,2,1,0:T(8,128)(2,1)S(1)}, f16[3,8,24,128]{3,2,1,0:T(8,128)(2,1)S(1)}, u32[]{:S(2)}, u32[]{:S(2)}) collective-permute-start(f16[3,8,24,128]{3,2,1,0:T(8,128)(2,1)S(1)} %bitcast.58), channel_id=1, source_target_pairs={{0,3},{1,2},{2,1},{3,0},{4,7},{5,6},{6,5},{7,4},{8,11},{9,10},{10,... | collective-permute-start | bytes 442376 | tf_op jit(solution)/shard_map/ppermute | solution.py:275
  12.3 0.0 collective-permute-start
  12.3 0.5 %collective-permute-done.6 = f32[200,128]{1,0:T(8,128)S(1)} collective-permute-done((f32[200,128]{1,0:T(8,128)S(1)}, f32[200,128]{1,0:T(8,128)S(1)}, u32[]{:S(2)}, u32[]{:S(2)}) %collective-permute-start.6) | collective-permute-done | bytes 102432 | tf_op jit(solution)/shard_map/ppermute | solution.py:275
  12.8 4.1 %collective-permute-done.1 = f16[3,8,24,128]{3,2,1,0:T(8,128)(2,1)S(1)} collective-permute-done((f16[3,8,24,128]{3,2,1,0:T(8,128)(2,1)S(1)}, f16[3,8,24,128]{3,2,1,0:T(8,128)(2,1)S(1)}, u32[]{:S(2)}, u32[]{:S(2)}) %collective-permute-start.1) | collective-permute-done | bytes 147488 | tf_op jit(solution)/shard_map/ppermute | solution.py:275
  16.9 0.1 multiply_convert_fusion.1
  17.1 0.2 collective-permute-start.4
  17.3 1.7 %collective-permute-start.3 = (f16[2,8,24,128]{3,2,1,0:T(8,128)(2,1)S(1)}, f16[2,8,24,128]{3,2,1,0:T(8,128)(2,1)S(1)}, u32[]{:S(2)}, u32[]{:S(2)}) collective-permute-start(f16[2,8,24,128]{3,2,1,0:T(8,128)(2,1)S(1)} %get-tuple-element.23), channel_id=1, source_target_pairs={{0,4},{4,0},{8,12},{12,8},{16,20},{20,16},{24,28},{28,24},{1,5},{5... | collective-permute-start | bytes 294920 | tf_op jit(solution)/shard_map/ppermute | solution.py:275
  19.0 2.7 %collective-permute-start.2 = (f16[2,8,24,128]{3,2,1,0:T(8,128)(2,1)S(1)}, f16[2,8,24,128]{3,2,1,0:T(8,128)(2,1)S(1)}, u32[]{:S(2)}, u32[]{:S(2)}) collective-permute-start(f16[2,8,24,128]{3,2,1,0:T(8,128)(2,1)S(1)} %get-tuple-element.24), channel_id=1, source_target_pairs={{0,28},{4,8},{8,4},{12,16},{16,12},{20,24},{24,20},{28,0},{1,29},{... | collective-permute-start | bytes 294920 | tf_op jit(solution)/shard_map/ppermute | solution.py:275
  21.7 0.3 collective-permute-done.4
  22.0 0.0 collective-permute-done.3
  22.1 3.1 %collective-permute-done.2 = f16[2,8,24,128]{3,2,1,0:T(8,128)(2,1)S(1)} collective-permute-done((f16[2,8,24,128]{3,2,1,0:T(8,128)(2,1)S(1)}, f16[2,8,24,128]{3,2,1,0:T(8,128)(2,1)S(1)}, u32[]{:S(2)}, u32[]{:S(2)}) %collective-permute-start.2) | collective-permute-done | bytes 98336 | tf_op jit(solution)/shard_map/ppermute | solution.py:275
  25.2 0.2 multiply_convert_fusion
  25.4 2.4 %collective-permute-start.9 = (bf16[3,8,24,128]{3,2,1,0:T(8,128)(2,1)S(1)}, bf16[3,8,24,128]{3,2,1,0:T(8,128)(2,1)S(1)}, u32[]{:S(2)}, u32[]{:S(2)}) collective-permute-start(bf16[3,8,24,128]{3,2,1,0:T(8,128)(2,1)S(1)} %get-tuple-element.16), channel_id=1, source_target_pairs={{0,1},{1,0},{2,3},{3,2},{4,5},{5,4},{6,7},{7,6},{8,9},{9,8},{10,11... | collective-permute-start | bytes 442376 | tf_op jit(solution)/shard_map/ppermute | solution.py:275
  27.9 0.7 %collective-permute-start.8 = (bf16[3,8,24,128]{3,2,1,0:T(8,128)(2,1)S(1)}, bf16[3,8,24,128]{3,2,1,0:T(8,128)(2,1)S(1)}, u32[]{:S(2)}, u32[]{:S(2)}) collective-permute-start(bf16[3,8,24,128]{3,2,1,0:T(8,128)(2,1)S(1)} %get-tuple-element.16), channel_id=1, source_target_pairs={{0,3},{1,2},{2,1},{3,0},{4,7},{5,6},{6,5},{7,4},{8,11},{9,10},{10,... | collective-permute-start | bytes 442376 | tf_op jit(solution)/shard_map/ppermute | solution.py:275
  28.5 0.6 %slice_bitcast_fusion = f32[8,24,128]{2,1,0:T(8,128)} fusion(f32[3,8,24,128]{3,2,1,0:T(8,128)S(1)} %get-tuple-element.17), kind=kLoop, calls=%fused_computation.10 | loop fusion | bytes 196608 | tf_op jit(solution)/shard_map/squeeze | solution.py:320
  29.2 4.2 %collective-permute-done.8 = bf16[3,8,24,128]{3,2,1,0:T(8,128)(2,1)S(1)} collective-permute-done((bf16[3,8,24,128]{3,2,1,0:T(8,128)(2,1)S(1)}, bf16[3,8,24,128]{3,2,1,0:T(8,128)(2,1)S(1)}, u32[]{:S(2)}, u32[]{:S(2)}) %collective-permute-start.8) | collective-permute-done | bytes 147488 | tf_op jit(solution)/shard_map/ppermute | solution.py:275
  33.4 0.1 pad_maximum_fusion
  33.5 2.5 %early_blocks.1 = (f32[3072,128]{1,0:T(8,128)S(1)}, s32[256]{0:T(256)S(1)}) custom-call(bf16[48,24,128]{2,1,0:T(8,128)(2,1)S(1)} %bitcast.43, bf16[192,128,128]{2,1,0:T(8,128)(2,1)S(1)} %bitcast.41, s32[2,1,192]{2,1,0:T(1,128)S(1)} %get-tuple-element.12.index_in), custom_call_target="tpu_custom_call" | custom-call | tf_op jit(solution)/shard_map/early_blocks/pallas_call | solution.py:228
  36.0 2.1 %backward_blocks.1 = (f32[3072,128]{1,0:T(8,128)S(1)}, f32[3072,128]{1,0:T(8,128)}) custom-call(bf16[72,24,128]{2,1,0:T(8,128)(2,1)S(1)} %bitcast.42, bf16[192,128,128]{2,1,0:T(8,128)(2,1)S(1)} %bitcast.41, s32[2,1,192]{2,1,0:T(1,128)S(1)} %get-tuple-element.12.index_in, s32[256]{0:T(256)S(1)} %get-tuple-element.13.order_in, ...), custom_call_target="tpu_custom_call", output_to_operand_aliasing={{0}: (4, {})} | custom-call | tf_op jit(solution)/shard_map/backward_blocks/pallas_call | solution.py:249
  (18 shorter events, 0.2 us)
Async XLA Ops:
  0.6 32.8 %slice-start = ((s8[6291456]{0:T(1024)(128)(4,1)}), s8[4194304]{0:T(1024)(128)(4,1)S(1)}, s32[]{:S(2)}) async-start(s8[6291456]{0:T(1024)(128)(4,1)} %bitcast.40), calls=%async_computation | async-start | bytes 8388608
  4.5 7.9 %collective-permute-start.7 = (f32[200,128]{1,0:T(8,128)S(1)}, f32[200,128]{1,0:T(8,128)S(1)}, u32[]{:S(2)}, u32[]{:S(2)}) collective-permute-start(f32[200,128]{1,0:T(8,128)S(1)} %get-tuple-element.11), channel_id=1, source_target_pairs={{0,4},{4,0},{8,12},{12,8},{16,20},{20,16},{24,28},{28,24},{1,5},{5... | collective-permute-start | bytes 307208 | tf_op jit(solution)/shard_map/ppermute | solution.py:275
  6.6 6.2 %collective-permute-start.6 = (f32[200,128]{1,0:T(8,128)S(1)}, f32[200,128]{1,0:T(8,128)S(1)}, u32[]{:S(2)}, u32[]{:S(2)}) collective-permute-start(f32[200,128]{1,0:T(8,128)S(1)} %get-tuple-element.11), channel_id=1, source_target_pairs={{0,28},{4,8},{8,4},{12,16},{16,12},{20,24},{24,20},{28,0},{1,29},{... | collective-permute-start | bytes 307208 | tf_op jit(solution)/shard_map/ppermute | solution.py:275
  9.9 23.6 %slice-start.1 = ((s8[6291456]{0:T(1024)(128)(4,1)}), s8[2097152]{0:T(1024)(128)(4,1)S(1)}, s32[]{:S(2)}) async-start(s8[6291456]{0:T(1024)(128)(4,1)} %bitcast.40), calls=%async_computation.1 | async-start | bytes 4194304
  9.9 7.0 %collective-permute-start.1 = (f16[3,8,24,128]{3,2,1,0:T(8,128)(2,1)S(1)}, f16[3,8,24,128]{3,2,1,0:T(8,128)(2,1)S(1)}, u32[]{:S(2)}, u32[]{:S(2)}) collective-permute-start(f16[3,8,24,128]{3,2,1,0:T(8,128)(2,1)S(1)} %bitcast.58), channel_id=1, source_target_pairs={{0,3},{1,2},{2,1},{3,0},{4,7},{5,6},{6,5},{7,4},{8,11},{9,10},{10,... | collective-permute-start | bytes 442376 | tf_op jit(solution)/shard_map/ppermute | solution.py:275
  12.3 4.6 %collective-permute-start = (f16[3,8,24,128]{3,2,1,0:T(8,128)(2,1)S(1)}, f16[3,8,24,128]{3,2,1,0:T(8,128)(2,1)S(1)}, u32[]{:S(2)}, u32[]{:S(2)}) collective-permute-start(f16[3,8,24,128]{3,2,1,0:T(8,128)(2,1)S(1)} %bitcast.57), channel_id=1, source_target_pairs={{0,1},{1,0},{2,3},{3,2},{4,5},{5,4},{6,7},{7,6},{8,9},{9,8},{10,11... | collective-permute-start | bytes 442376 | tf_op jit(solution)/shard_map/ppermute | solution.py:275
  17.1 4.9 %collective-permute-start.4 = (f16[8,24,128]{2,1,0:T(8,128)(2,1)S(1)}, f16[8,24,128]{2,1,0:T(8,128)(2,1)S(1)}, u32[]{:S(2)}, u32[]{:S(2)}) collective-permute-start(f16[8,24,128]{2,1,0:T(8,128)(2,1)S(1)} %get-tuple-element.21), channel_id=1, source_target_pairs={{0,24},{4,28},{8,16},{12,20},{16,8},{20,12},{24,0},{28,4},{1,25},{... | collective-permute-start | bytes 147464 | tf_op jit(solution)/shard_map/ppermute | solution.py:275
  17.3 4.7 %collective-permute-start.5 = (f16[8,24,128]{2,1,0:T(8,128)(2,1)S(1)}, f16[8,24,128]{2,1,0:T(8,128)(2,1)S(1)}, u32[]{:S(2)}, u32[]{:S(2)}) collective-permute-start(f16[8,24,128]{2,1,0:T(8,128)(2,1)S(1)} %get-tuple-element.22), channel_id=1, source_target_pairs={{0,8},{4,12},{8,0},{12,4},{16,24},{20,28},{24,16},{28,20},{1,9},{5... | collective-permute-start | bytes 147464 | tf_op jit(solution)/shard_map/ppermute | solution.py:275
  17.3 4.7 %collective-permute-start.3 = (f16[2,8,24,128]{3,2,1,0:T(8,128)(2,1)S(1)}, f16[2,8,24,128]{3,2,1,0:T(8,128)(2,1)S(1)}, u32[]{:S(2)}, u32[]{:S(2)}) collective-permute-start(f16[2,8,24,128]{3,2,1,0:T(8,128)(2,1)S(1)} %get-tuple-element.23), channel_id=1, source_target_pairs={{0,4},{4,0},{8,12},{12,8},{16,20},{20,16},{24,28},{28,24},{1,5},{5... | collective-permute-start | bytes 294920 | tf_op jit(solution)/shard_map/ppermute | solution.py:275
  19.0 6.2 %collective-permute-start.2 = (f16[2,8,24,128]{3,2,1,0:T(8,128)(2,1)S(1)}, f16[2,8,24,128]{3,2,1,0:T(8,128)(2,1)S(1)}, u32[]{:S(2)}, u32[]{:S(2)}) collective-permute-start(f16[2,8,24,128]{3,2,1,0:T(8,128)(2,1)S(1)} %get-tuple-element.24), channel_id=1, source_target_pairs={{0,28},{4,8},{8,4},{12,16},{16,12},{20,24},{24,20},{28,0},{1,29},{... | collective-permute-start | bytes 294920 | tf_op jit(solution)/shard_map/ppermute | solution.py:275
  25.4 3.8 %collective-permute-start.9 = (bf16[3,8,24,128]{3,2,1,0:T(8,128)(2,1)S(1)}, bf16[3,8,24,128]{3,2,1,0:T(8,128)(2,1)S(1)}, u32[]{:S(2)}, u32[]{:S(2)}) collective-permute-start(bf16[3,8,24,128]{3,2,1,0:T(8,128)(2,1)S(1)} %get-tuple-element.16), channel_id=1, source_target_pairs={{0,1},{1,0},{2,3},{3,2},{4,5},{5,4},{6,7},{7,6},{8,9},{9,8},{10,11... | collective-permute-start | bytes 442376 | tf_op jit(solution)/shard_map/ppermute | solution.py:275
  27.9 5.5 %collective-permute-start.8 = (bf16[3,8,24,128]{3,2,1,0:T(8,128)(2,1)S(1)}, bf16[3,8,24,128]{3,2,1,0:T(8,128)(2,1)S(1)}, u32[]{:S(2)}, u32[]{:S(2)}) collective-permute-start(bf16[3,8,24,128]{3,2,1,0:T(8,128)(2,1)S(1)} %get-tuple-element.16), channel_id=1, source_target_pairs={{0,3},{1,2},{2,1},{3,0},{4,7},{5,6},{6,5},{7,4},{8,11},{9,10},{10,... | collective-permute-start | bytes 442376 | tf_op jit(solution)/shard_map/ppermute | solution.py:275

commit v5 on v4

--- a/solution.py
+++ b/solution.py
@@ -124,7 +124,7 @@
 
 
 def run_step(count):
-    return next(step for step in (48, 16, 8, 4) if count % step == 0)
+    return next(step for step in (24, 16, 8, 4) if count % step == 0)
 
 
 def run_blocks(first, last, near, blocks, index, order, total, skipped):
@@ -142,6 +142,23 @@
     lax.fori_loop(first, last, trip, 0)
 
 
+def run_pairs(first, last, near, blocks, index, order, total):
+    rows = near.shape[1]
+    step = run_step(blocks.shape[0])
+    odd = (last - first) % 2
+
+    def trip(at, carry):
+        block_sums(
+            (first + odd + 2 * at) * step, 2 * step, lambda b: order[b],
+            lambda b, c: jnp.concatenate([blocks[b], blocks[c]], axis=0), lambda s: near[s],
+            lambda b: index[0, 0, b], lambda b: index[1, 0, b], total, rows,
+        )
+        return carry
+
+    run_blocks(first, first + odd, near, blocks, index, order, total, 0)
+    lax.fori_loop(0, (last - first) // 2, trip, 0)
+
+
 def early_kernel(tiles, near, blocks, index_in, total, order_out, index, order, sems):
     count = blocks.shape[0]
     outer = 3 * tiles
@@ -172,7 +189,7 @@
     )
     for copy in copies:
         copy.wait()
-    run_blocks(order[count], count // run_step(count), near, blocks, index, order, total, 0)
+    run_pairs(order[count], count // run_step(count), near, blocks, index, order, total)
     result = pltpu.make_async_copy(total, out, sems.at[0])
     result.start()
     result.wait()

time: 38.4 us -> 38.8 us (1.010)
  Pallas kernels: 8.49 us -> 8.91 us
    pallas_call x1, Pallas kernels: 2.52 us -> 2.92 us  [backward_early(): pl.pallas_call(functools.partial(early_kernel, tiles), out_shape=[jax.Sha...]
where the time goes in v5:
time: 38.8 us; the launch traced here: 38.6 us
  starting transfers between devices  15.5 us (40%)
  waiting for transfers between devices  12.2 us (31%)
  Pallas kernels  8.91 us (23%)
  between operations  0.76 us (2%)
  local copies, waits for them, and re-layouts  0.74 us (2%)
  other arithmetic  0.5 us (1%)
    ppermute x10, starting transfers between devices, swap(): lax.ppermute(block, axis, ring_pairs(lax.axis_size(axis), stride, inner))  15.5 us
    ppermute x10, waiting for transfers between devices, swap(): lax.ppermute(block, axis, ring_pairs(lax.axis_size(axis), stride, inner))  12.2 us
    pallas_call x1, Pallas kernels, forward(): pl.pallas_call(functools.partial(fwd_kernel, n_atmos, n_ocean), out_shape...  3.82 us
    pallas_call x1, Pallas kernels, backward_early(): pl.pallas_call(functools.partial(early_kernel, tiles), out_shape=[jax.Sha...  2.92 us
    pallas_call x1, Pallas kernels, backward_late(): pl.pallas_call(late_kernel, out_shape=[shape, shape], in_specs=[vmem()] *...  2.17 us
  transfers between devices with their start and end apart: 10, of which 5 were waited for; matrix products, arithmetic and copies ran while one was open for 2% of the time, Pallas kernels for 0%

profile of v5, /device:TPU:1, one launch (start us, length us, event | category | flops | bytes accessed | tf_op | source)
XLA Modules:
  0.0 38.6 jit_solution(6258882833954114108)
XLA Ops:
  0.6 0.0 slice-start
  0.6 3.8 %forward_blocks.1 = (f32[1728,128]{1,0:T(8,128)S(1)}, f32[200,128]{1,0:T(8,128)S(1)}, s32[2,1,192]{2,1,0:T(1,128)S(1)}, s32[1,1,128]{2,1,0:T(1,128)S(1)}) custom-call(bf16[128,24,128]{2,1,0:T(8,128)(2,1)} %fields_hbm.1, bf16[192,128,128]{2,1,0:T(8,128)(2,1)} %blocks_hbm.1, s32[1,192]{1,0:T(1,128)} %bitcast.61, s32[1,192]{1,0:T(1,128)} %bitcast.62, ...), custom_call_target="tpu_custom_call" | custom-call | tf_op jit(solution)/shard_map/forward_blocks/pallas_call | solution.py:216
  4.5 2.1 %collective-permute-start.7 = (f32[200,128]{1,0:T(8,128)S(1)}, f32[200,128]{1,0:T(8,128)S(1)}, u32[]{:S(2)}, u32[]{:S(2)}) collective-permute-start(f32[200,128]{1,0:T(8,128)S(1)} %get-tuple-element.11), channel_id=1, source_target_pairs={{0,4},{4,0},{8,12},{12,8},{16,20},{20,16},{24,28},{28,24},{1,5},{5... | collective-permute-start | bytes 307208 | tf_op jit(solution)/shard_map/ppermute | solution.py:292
  6.6 3.3 %collective-permute-start.6 = (f32[200,128]{1,0:T(8,128)S(1)}, f32[200,128]{1,0:T(8,128)S(1)}, u32[]{:S(2)}, u32[]{:S(2)}) collective-permute-start(f32[200,128]{1,0:T(8,128)S(1)} %get-tuple-element.11), channel_id=1, source_target_pairs={{0,28},{4,8},{8,4},{12,16},{16,12},{20,24},{24,20},{28,0},{1,29},{... | collective-permute-start | bytes 307208 | tf_op jit(solution)/shard_map/ppermute | solution.py:292
  9.9 0.1 multiply_convert_fusion.3
  9.9 2.4 %collective-permute-start.1 = (f16[3,8,24,128]{3,2,1,0:T(8,128)(2,1)S(1)}, f16[3,8,24,128]{3,2,1,0:T(8,128)(2,1)S(1)}, u32[]{:S(2)}, u32[]{:S(2)}) collective-permute-start(f16[3,8,24,128]{3,2,1,0:T(8,128)(2,1)S(1)} %bitcast.58), channel_id=1, source_target_pairs={{0,3},{1,2},{2,1},{3,0},{4,7},{5,6},{6,5},{7,4},{8,11},{9,10},{10,... | collective-permute-start | bytes 442376 | tf_op jit(solution)/shard_map/ppermute | solution.py:292
  12.3 0.0 collective-permute-start
  12.3 0.5 %collective-permute-done.6 = f32[200,128]{1,0:T(8,128)S(1)} collective-permute-done((f32[200,128]{1,0:T(8,128)S(1)}, f32[200,128]{1,0:T(8,128)S(1)}, u32[]{:S(2)}, u32[]{:S(2)}) %collective-permute-start.6) | collective-permute-done | bytes 102432 | tf_op jit(solution)/shard_map/ppermute | solution.py:292
  12.8 4.1 %collective-permute-done.1 = f16[3,8,24,128]{3,2,1,0:T(8,128)(2,1)S(1)} collective-permute-done((f16[3,8,24,128]{3,2,1,0:T(8,128)(2,1)S(1)}, f16[3,8,24,128]{3,2,1,0:T(8,128)(2,1)S(1)}, u32[]{:S(2)}, u32[]{:S(2)}) %collective-permute-start.1) | collective-permute-done | bytes 147488 | tf_op jit(solution)/shard_map/ppermute | solution.py:292
  16.9 0.1 multiply_convert_fusion.1
  17.1 0.2 collective-permute-start.4
  17.3 1.7 %collective-permute-start.3 = (f16[2,8,24,128]{3,2,1,0:T(8,128)(2,1)S(1)}, f16[2,8,24,128]{3,2,1,0:T(8,128)(2,1)S(1)}, u32[]{:S(2)}, u32[]{:S(2)}) collective-permute-start(f16[2,8,24,128]{3,2,1,0:T(8,128)(2,1)S(1)} %get-tuple-element.23), channel_id=1, source_target_pairs={{0,4},{4,0},{8,12},{12,8},{16,20},{20,16},{24,28},{28,24},{1,5},{5... | collective-permute-start | bytes 294920 | tf_op jit(solution)/shard_map/ppermute | solution.py:292
  19.0 2.7 %collective-permute-start.2 = (f16[2,8,24,128]{3,2,1,0:T(8,128)(2,1)S(1)}, f16[2,8,24,128]{3,2,1,0:T(8,128)(2,1)S(1)}, u32[]{:S(2)}, u32[]{:S(2)}) collective-permute-start(f16[2,8,24,128]{3,2,1,0:T(8,128)(2,1)S(1)} %get-tuple-element.24), channel_id=1, source_target_pairs={{0,28},{4,8},{8,4},{12,16},{16,12},{20,24},{24,20},{28,0},{1,29},{... | collective-permute-start | bytes 294920 | tf_op jit(solution)/shard_map/ppermute | solution.py:292
  21.7 0.3 collective-permute-done.4
  22.0 0.0 collective-permute-done.3
  22.1 3.1 %collective-permute-done.2 = f16[2,8,24,128]{3,2,1,0:T(8,128)(2,1)S(1)} collective-permute-done((f16[2,8,24,128]{3,2,1,0:T(8,128)(2,1)S(1)}, f16[2,8,24,128]{3,2,1,0:T(8,128)(2,1)S(1)}, u32[]{:S(2)}, u32[]{:S(2)}) %collective-permute-start.2) | collective-permute-done | bytes 98336 | tf_op jit(solution)/shard_map/ppermute | solution.py:292
  25.2 0.2 multiply_convert_fusion
  25.4 2.4 %collective-permute-start.9 = (bf16[3,8,24,128]{3,2,1,0:T(8,128)(2,1)S(1)}, bf16[3,8,24,128]{3,2,1,0:T(8,128)(2,1)S(1)}, u32[]{:S(2)}, u32[]{:S(2)}) collective-permute-start(bf16[3,8,24,128]{3,2,1,0:T(8,128)(2,1)S(1)} %get-tuple-element.16), channel_id=1, source_target_pairs={{0,1},{1,0},{2,3},{3,2},{4,5},{5,4},{6,7},{7,6},{8,9},{9,8},{10,11... | collective-permute-start | bytes 442376 | tf_op jit(solution)/shard_map/ppermute | solution.py:292
  27.9 0.7 %collective-permute-start.8 = (bf16[3,8,24,128]{3,2,1,0:T(8,128)(2,1)S(1)}, bf16[3,8,24,128]{3,2,1,0:T(8,128)(2,1)S(1)}, u32[]{:S(2)}, u32[]{:S(2)}) collective-permute-start(bf16[3,8,24,128]{3,2,1,0:T(8,128)(2,1)S(1)} %get-tuple-element.16), channel_id=1, source_target_pairs={{0,3},{1,2},{2,1},{3,0},{4,7},{5,6},{6,5},{7,4},{8,11},{9,10},{10,... | collective-permute-start | bytes 442376 | tf_op jit(solution)/shard_map/ppermute | solution.py:292
  28.5 0.6 %slice_bitcast_fusion = f32[8,24,128]{2,1,0:T(8,128)} fusion(f32[3,8,24,128]{3,2,1,0:T(8,128)S(1)} %get-tuple-element.17), kind=kLoop, calls=%fused_computation.10 | loop fusion | bytes 196608 | tf_op jit(solution)/shard_map/squeeze | solution.py:337
  29.2 4.2 %collective-permute-done.8 = bf16[3,8,24,128]{3,2,1,0:T(8,128)(2,1)S(1)} collective-permute-done((bf16[3,8,24,128]{3,2,1,0:T(8,128)(2,1)S(1)}, bf16[3,8,24,128]{3,2,1,0:T(8,128)(2,1)S(1)}, u32[]{:S(2)}, u32[]{:S(2)}) %collective-permute-start.8) | collective-permute-done | bytes 147488 | tf_op jit(solution)/shard_map/ppermute | solution.py:292
  33.4 0.1 pad_maximum_fusion
  33.5 2.9 %early_blocks.1 = (f32[3072,128]{1,0:T(8,128)S(1)}, s32[256]{0:T(256)S(1)}) custom-call(bf16[48,24,128]{2,1,0:T(8,128)(2,1)S(1)} %bitcast.43, bf16[192,128,128]{2,1,0:T(8,128)(2,1)S(1)} %bitcast.41, s32[2,1,192]{2,1,0:T(1,128)S(1)} %get-tuple-element.12.index_in), custom_call_target="tpu_custom_call" | custom-call | tf_op jit(solution)/shard_map/early_blocks/pallas_call | solution.py:245
  36.4 2.2 %backward_blocks.1 = (f32[3072,128]{1,0:T(8,128)S(1)}, f32[3072,128]{1,0:T(8,128)}) custom-call(bf16[72,24,128]{2,1,0:T(8,128)(2,1)S(1)} %bitcast.42, bf16[192,128,128]{2,1,0:T(8,128)(2,1)S(1)} %bitcast.41, s32[2,1,192]{2,1,0:T(1,128)S(1)} %get-tuple-element.12.index_in, s32[256]{0:T(256)S(1)} %get-tuple-element.13.order_in, ...), custom_call_target="tpu_custom_call", output_to_operand_aliasing={{0}: (4, {})} | custom-call | tf_op jit(solution)/shard_map/backward_blocks/pallas_call | solution.py:266
  (18 shorter events, 0.2 us)
Async XLA Ops:
  0.6 32.8 %slice-start = ((s8[6291456]{0:T(1024)(128)(4,1)}), s8[4194304]{0:T(1024)(128)(4,1)S(1)}, s32[]{:S(2)}) async-start(s8[6291456]{0:T(1024)(128)(4,1)} %bitcast.40), calls=%async_computation | async-start | bytes 8388608
  4.5 7.9 %collective-permute-start.7 = (f32[200,128]{1,0:T(8,128)S(1)}, f32[200,128]{1,0:T(8,128)S(1)}, u32[]{:S(2)}, u32[]{:S(2)}) collective-permute-start(f32[200,128]{1,0:T(8,128)S(1)} %get-tuple-element.11), channel_id=1, source_target_pairs={{0,4},{4,0},{8,12},{12,8},{16,20},{20,16},{24,28},{28,24},{1,5},{5... | collective-permute-start | bytes 307208 | tf_op jit(solution)/shard_map/ppermute | solution.py:292
  6.6 6.2 %collective-permute-start.6 = (f32[200,128]{1,0:T(8,128)S(1)}, f32[200,128]{1,0:T(8,128)S(1)}, u32[]{:S(2)}, u32[]{:S(2)}) collective-permute-start(f32[200,128]{1,0:T(8,128)S(1)} %get-tuple-element.11), channel_id=1, source_target_pairs={{0,28},{4,8},{8,4},{12,16},{16,12},{20,24},{24,20},{28,0},{1,29},{... | collective-permute-start | bytes 307208 | tf_op jit(solution)/shard_map/ppermute | solution.py:292
  9.9 23.6 %slice-start.1 = ((s8[6291456]{0:T(1024)(128)(4,1)}), s8[2097152]{0:T(1024)(128)(4,1)S(1)}, s32[]{:S(2)}) async-start(s8[6291456]{0:T(1024)(128)(4,1)} %bitcast.40), calls=%async_computation.1 | async-start | bytes 4194304
  9.9 7.0 %collective-permute-start.1 = (f16[3,8,24,128]{3,2,1,0:T(8,128)(2,1)S(1)}, f16[3,8,24,128]{3,2,1,0:T(8,128)(2,1)S(1)}, u32[]{:S(2)}, u32[]{:S(2)}) collective-permute-start(f16[3,8,24,128]{3,2,1,0:T(8,128)(2,1)S(1)} %bitcast.58), channel_id=1, source_target_pairs={{0,3},{1,2},{2,1},{3,0},{4,7},{5,6},{6,5},{7,4},{8,11},{9,10},{10,... | collective-permute-start | bytes 442376 | tf_op jit(solution)/shard_map/ppermute | solution.py:292
  12.3 4.6 %collective-permute-start = (f16[3,8,24,128]{3,2,1,0:T(8,128)(2,1)S(1)}, f16[3,8,24,128]{3,2,1,0:T(8,128)(2,1)S(1)}, u32[]{:S(2)}, u32[]{:S(2)}) collective-permute-start(f16[3,8,24,128]{3,2,1,0:T(8,128)(2,1)S(1)} %bitcast.57), channel_id=1, source_target_pairs={{0,1},{1,0},{2,3},{3,2},{4,5},{5,4},{6,7},{7,6},{8,9},{9,8},{10,11... | collective-permute-start | bytes 442376 | tf_op jit(solution)/shard_map/ppermute | solution.py:292
  17.1 4.9 %collective-permute-start.4 = (f16[8,24,128]{2,1,0:T(8,128)(2,1)S(1)}, f16[8,24,128]{2,1,0:T(8,128)(2,1)S(1)}, u32[]{:S(2)}, u32[]{:S(2)}) collective-permute-start(f16[8,24,128]{2,1,0:T(8,128)(2,1)S(1)} %get-tuple-element.21), channel_id=1, source_target_pairs={{0,24},{4,28},{8,16},{12,20},{16,8},{20,12},{24,0},{28,4},{1,25},{... | collective-permute-start | bytes 147464 | tf_op jit(solution)/shard_map/ppermute | solution.py:292
  17.3 4.7 %collective-permute-start.5 = (f16[8,24,128]{2,1,0:T(8,128)(2,1)S(1)}, f16[8,24,128]{2,1,0:T(8,128)(2,1)S(1)}, u32[]{:S(2)}, u32[]{:S(2)}) collective-permute-start(f16[8,24,128]{2,1,0:T(8,128)(2,1)S(1)} %get-tuple-element.22), channel_id=1, source_target_pairs={{0,8},{4,12},{8,0},{12,4},{16,24},{20,28},{24,16},{28,20},{1,9},{5... | collective-permute-start | bytes 147464 | tf_op jit(solution)/shard_map/ppermute | solution.py:292
  17.3 4.7 %collective-permute-start.3 = (f16[2,8,24,128]{3,2,1,0:T(8,128)(2,1)S(1)}, f16[2,8,24,128]{3,2,1,0:T(8,128)(2,1)S(1)}, u32[]{:S(2)}, u32[]{:S(2)}) collective-permute-start(f16[2,8,24,128]{3,2,1,0:T(8,128)(2,1)S(1)} %get-tuple-element.23), channel_id=1, source_target_pairs={{0,4},{4,0},{8,12},{12,8},{16,20},{20,16},{24,28},{28,24},{1,5},{5... | collective-permute-start | bytes 294920 | tf_op jit(solution)/shard_map/ppermute | solution.py:292
  19.0 6.2 %collective-permute-start.2 = (f16[2,8,24,128]{3,2,1,0:T(8,128)(2,1)S(1)}, f16[2,8,24,128]{3,2,1,0:T(8,128)(2,1)S(1)}, u32[]{:S(2)}, u32[]{:S(2)}) collective-permute-start(f16[2,8,24,128]{3,2,1,0:T(8,128)(2,1)S(1)} %get-tuple-element.24), channel_id=1, source_target_pairs={{0,28},{4,8},{8,4},{12,16},{16,12},{20,24},{24,20},{28,0},{1,29},{... | collective-permute-start | bytes 294920 | tf_op jit(solution)/shard_map/ppermute | solution.py:292
  25.4 3.8 %collective-permute-start.9 = (bf16[3,8,24,128]{3,2,1,0:T(8,128)(2,1)S(1)}, bf16[3,8,24,128]{3,2,1,0:T(8,128)(2,1)S(1)}, u32[]{:S(2)}, u32[]{:S(2)}) collective-permute-start(bf16[3,8,24,128]{3,2,1,0:T(8,128)(2,1)S(1)} %get-tuple-element.16), channel_id=1, source_target_pairs={{0,1},{1,0},{2,3},{3,2},{4,5},{5,4},{6,7},{7,6},{8,9},{9,8},{10,11... | collective-permute-start | bytes 442376 | tf_op jit(solution)/shard_map/ppermute | solution.py:292
  27.9 5.5 %collective-permute-start.8 = (bf16[3,8,24,128]{3,2,1,0:T(8,128)(2,1)S(1)}, bf16[3,8,24,128]{3,2,1,0:T(8,128)(2,1)S(1)}, u32[]{:S(2)}, u32[]{:S(2)}) collective-permute-start(bf16[3,8,24,128]{3,2,1,0:T(8,128)(2,1)S(1)} %get-tuple-element.16), channel_id=1, source_target_pairs={{0,3},{1,2},{2,1},{3,0},{4,7},{5,6},{6,5},{7,4},{8,11},{9,10},{10,... | collective-permute-start | bytes 442376 | tf_op jit(solution)/shard_map/ppermute | solution.py:292
